TPU v7x, 32 devices: a whole 2x2x4 slice. The times are simulated.
32 devices in a mesh: groups: 2 (over y), tm: 4 (over z), head: 4 (over x, core).
Axes of the slice: x: 2, y: 2, z: 4, core: 2. Of those that a mesh axis runs over, the one named last changes fastest.
Arguments:
- queries: bfloat16 [8, 256, 3072], P(('groups', 'tm'), 'head'), parts along dimension 0, may hold values from -128 to 128
- keys: bfloat16 [8, 256, 3072], P(('groups', 'tm'), 'head'), parts along dimension 0, may hold values from -6 to 6
- values: bfloat16 [8, 256, 3072], P(('groups', 'tm'), 'head'), parts along dimension 0, may hold values from -6 to 6
- residual: bfloat16 [8, 256, 5120], P(('groups', 'tm'), None, 'head'), parts along dimension 0, may hold values from -3 to 3
- fresh_frame: bfloat16 [512, 5120], P('groups', 'head'), parts along dimension 0, may hold values from -6 to 6
- out_weight: bfloat16 [3072, 5120], P('tm', 'head'), may hold values from -0.875 to 0.875
- time_weight: bfloat16 [256, 5120], P(None, 'head'), may hold values from -0.375 to 0.375
- noise_steps: int32 [8], P(('groups', 'tm')), parts along dimension 0, may hold values from 0 to 49, as said below
- frame_mask: int32 [8, 4], P(('groups', 'tm')), parts along dimension 0, may hold values from 0 to 1, as said below
Outputs:
- rolled: bfloat16 [8, 256, 5120], P(('groups', 'tm'), None, 'head'), parts along dimension 0
There are 2 independent parts, one for each index of `groups`. A program takes and returns all parts, laid end to end along the dimension named above; an argument that names none is the same for every part. Nothing has to cross between parts.
Inputs may be any that keep to these rules, and one draw needn't show every extreme that they name: frame_mask[i, j] is 1 exactly for i - L_i < j <= i, with a whole number L_i from 1 to 4 for each frame i; the last frame has L_i = 4. `noise_steps`: never falling along the frames; the first frame has 0 and the last 49.
All inputs are finite; a program needn't handle non-finite values.
Results may differ from a plain program's by a relative error of at most 0.0065.
Values may be sent and summed in bfloat16 or wider, within the bound.
A program may use at most 64 MiB of HBM per device.

v0:
```python
import functools
import math

import jax
import jax.numpy as jnp
from jax import lax
from jax.experimental import pallas as pl
from jax.experimental.pallas import tpu as pltpu
from jax.sharding import PartitionSpec as P

HD = 128
FREQ = 256
STEPS = 50


def shifted(value, axis, steps):
    count = lax.axis_size(axis)
    leading, last = (max(0, -steps), min(count, count - steps))
    return lax.ppermute(value, axis, [(source, source + steps) for source in range(leading, last)])


def time_features(noise_steps):
    timestep = 1000.0 * (noise_steps.astype(jnp.float32) + 1.0) / STEPS
    half = FREQ // 2
    rates = jnp.exp(-math.log(10000.0) * jnp.arange(half).astype(jnp.float32) / half)
    angles = timestep[:, None] * rates[None, :]
    return jnp.concatenate([jnp.cos(angles), jnp.sin(angles)], axis=1)


def on_device(
    queries, keys, values, residual, fresh_frame, out_weight, time_weight, noise_steps, frame_mask
):
    query_local, key_local, value_local = (
        lax.all_to_all(queries, "head", split_axis=2, concat_axis=1, tiled=True),
        lax.all_to_all(keys, "head", split_axis=2, concat_axis=1, tiled=True),
        lax.all_to_all(values, "head", split_axis=2, concat_axis=1, tiled=True),
    )
    tokens = query_local.shape[1]
    heads_here = query_local.shape[2] // HD
    scale = 1.0 / math.sqrt(HD)
    query_heads = query_local[0].reshape(tokens, heads_here, HD)
    key_value = jnp.stack([key_local[0], value_local[0]], axis=0)
    frame = lax.axis_index("tm")
    frames_total = lax.axis_size("tm")
    window = min(8, frames_total)
    mask_row = frame_mask[0]
    columns = jnp.arange(mask_row.shape[0], dtype=jnp.int32)

    def allowed_at(offset):
        hits = jnp.sum(jnp.where(columns == frame - offset, mask_row, 0))
        return hits > 0

    def absorb(state, block, allowed):
        running_max, weight_sum, accumulated = state
        key_heads = block[0].reshape(tokens, heads_here, HD)
        value_heads = block[1].reshape(tokens, heads_here, HD)
        scores = (
            jnp.einsum("qhd,khd->hqk", query_heads, key_heads, preferred_element_type=jnp.float32)
            * scale
        )
        new_max = jnp.where(allowed, jnp.maximum(running_max, jnp.max(scores, axis=2)), running_max)
        lifted = jnp.where(allowed, jnp.exp(jnp.minimum(scores - new_max[:, :, None], 0.0)), 0.0)
        factor = jnp.exp(running_max - new_max)
        weight_sum = weight_sum * factor + jnp.sum(lifted, axis=2)
        rounded = lifted.astype(jnp.bfloat16)
        accumulated = accumulated * jnp.transpose(factor)[:, :, None] + jnp.einsum(
            "hqk,khd->qhd", rounded, value_heads, preferred_element_type=jnp.float32
        )
        return (new_max, weight_sum, accumulated)

    state = (
        jnp.full((heads_here, tokens), -1e30, jnp.float32),
        jnp.zeros((heads_here, tokens), jnp.float32),
        jnp.zeros((tokens, heads_here, HD), jnp.float32),
    )
    state = absorb(state, key_value, allowed_at(0))
    moving = key_value
    for offset in range(1, window):
        moving = shifted(moving, "tm", 1)
        state = absorb(state, moving, allowed_at(offset))
    running_max, weight_sum, accumulated = state
    attention = (
        (accumulated / jnp.transpose(weight_sum)[:, :, None])
        .reshape(tokens, heads_here * HD)
        .astype(jnp.bfloat16)
    )
    weight_cols = lax.all_gather(out_weight, "tm", axis=0, tiled=True)
    projected = jnp.dot(
        lax.all_gather(attention, "head", axis=1, tiled=True),
        weight_cols,
        preferred_element_type=jnp.float32,
    )
    gate = jnp.dot(
        time_features(noise_steps), time_weight.astype(jnp.float32), precision=lax.Precision.HIGHEST
    )
    updated = (residual[0].astype(jnp.float32) + gate * projected).astype(jnp.bfloat16)
    moved = shifted(updated, "tm", -1)
    rolled = jnp.where(frame == frames_total - 1, fresh_frame, moved)
    return rolled[None]


def fused_kernel(
    T, G, C, hp, pieces, kept, groups,
    q_ref, k_ref, v_ref, res_ref, fresh_ref, w_ref, tw_ref, meta_ref,
    out_ref,
    qb, kb, vb, ab, mb, fb, gb, wb, twb, rb, pb, down_out, down_in, up_out, up_in, ab3, w3,
    load_sem, meta_send, meta_recv, qkv_send, qkv_recv, pass_send, pass_recv,
    ax_send, ax_recv, ac_send, ac_recv, dn_send, dn_recv, up_send, up_recv,
    w_send, w_recv, l_send, l_recv, lx_send, lx_recv, lc_send, lc_recv,
):
    t = lax.axis_index("tm")
    h = lax.axis_index("head")
    x = h // C
    c = lax.rem(h, C)
    H = G * C
    tl = q_ref.shape[1]
    cw = hp * HD
    tokens = tl * H
    half = G * tl
    nb = w_ref.shape[1] // pieces
    mask_row = FREQ // HD

    def to(tt, hh):
        return dict(device_id={"tm": tt, "head": hh}, device_id_type=pl.DeviceIdType.MESH)

    group = lax.axis_index("groups")
    share = w_ref.shape[0] // groups

    def beside(dg):
        return dict(
            device_id={"groups": lax.rem(group + dg, groups)}, device_id_type=pl.DeviceIdType.MESH
        )

    def landed(ref, sem):
        pltpu.make_async_copy(ref, ref, sem).wait()

    others = [(dt, dx) for dt in range(T) for dx in reversed(range(G)) if (dt, dx) != (0, 0)]

    loads = [
        pltpu.make_async_copy(w_ref, wb, load_sem.at[0]),
        pltpu.make_async_copy(res_ref.at[0], rb, load_sem.at[1]),
        pltpu.make_async_copy(tw_ref, twb, load_sem.at[2]),
    ]
    for copy in loads:
        copy.start()

    barrier = pltpu.get_barrier_semaphore()
    for dt, dx in others:
        pl.semaphore_signal(
            barrier, inc=1, **to(lax.rem(t + dt, T), lax.rem(x + dx, G) * C + c)
        )
    for dc in range(1, C):
        pl.semaphore_signal(barrier, inc=1, **to(t, x * C + lax.rem(c + dc, C)))
    for dg in range(1, groups):
        pl.semaphore_signal(barrier, inc=1, **beside(dg))
    pl.semaphore_wait(barrier, len(others) + C - 1 + groups - 1)

    own_meta = pltpu.make_async_copy(meta_ref, mb.at[t], meta_recv.at[t])
    own_meta.start()
    meta_copies = []
    for dt in range(1, T):
        meta_copies.append(
            pltpu.make_async_remote_copy(
                src_ref=meta_ref, dst_ref=mb.at[t], send_sem=meta_send.at[dt],
                recv_sem=meta_recv.at[t], **to(lax.rem(t + dt, T), h),
            )
        )
        meta_copies[-1].start()

    sources = ((q_ref, qb), (k_ref, kb), (v_ref, vb))

    def slot(kind, f, xs):
        return qb.at[f, xs] if kind == 0 else sources[kind][1].at[f, xs * C + c]

    def block(kind, tt, xx):
        column = pl.multiple_of((tt * G + xx) * cw, HD)
        return sources[kind][0].at[0, :, pl.ds(column, cw)]

    def outgoing(kind, dt, dx):
        tt, xx = lax.rem(t + dt, T), lax.rem(x + dx, G)
        return pltpu.make_async_remote_copy(
            src_ref=block(kind, tt, xx), dst_ref=slot(kind, t, x),
            send_sem=qkv_send.at[kind, dt, dx], recv_sem=qkv_recv.at[kind, t, x],
            **to(tt, xx * C + c),
        )

    def own(kind):
        return pltpu.make_async_copy(block(kind, t, x), slot(kind, t, x), qkv_recv.at[kind, t, x])

    def each_outgoing(act):
        for dt, dx in others:
            for kind in (1, 2):
                act(outgoing(kind, dt, dx))

            @pl.when(t > 0)
            def _():
                act(outgoing(0, dt, dx))

    own_rows = pl.ds(group * share, share)

    def lift_weight():
        return pltpu.make_async_remote_copy(
            src_ref=w_ref.at[own_rows, pl.ds(kept * nb, w3.shape[1])], dst_ref=w3.at[own_rows],
            send_sem=w_send.at[0], recv_sem=w_recv.at[0], **to(t - 1, h),
        )

    def trade_weight(dg):
        return pltpu.make_async_remote_copy(
            src_ref=w3.at[own_rows], dst_ref=w3.at[own_rows],
            send_sem=w_send.at[dg], recv_sem=w_recv.at[dg], **beside(dg),
        )

    @pl.when(t == T - 1)
    def _():
        lift_weight().start()

    each_outgoing(lambda copy: copy.start())
    for kind in (1, 2):
        own(kind).start()

    @pl.when(t > 0)
    def _():
        own(0).start()

    def passed(kind, dc, f, xs):
        return pltpu.make_async_remote_copy(
            src_ref=slot(kind, f, xs), dst_ref=slot(kind, f, xs),
            send_sem=pass_send.at[kind - 1, dc, f, xs], recv_sem=pass_recv.at[kind - 1, dc, f, xs],
            **to(t, x * C + lax.rem(c + dc, C)),
        )

    for copy in loads:
        copy.wait()
    fb[...] = jnp.zeros_like(fb)
    for f in range(T):
        landed(mb.at[f], meta_recv.at[f])
        for b in range(mask_row):
            fb[f : f + 1, b * HD : (b + 1) * HD] = mb[f, b : b + 1, :]
    gb[...] = jnp.dot(
        fb[...], twb[...].astype(jnp.float32),
        precision=lax.Precision.HIGHEST, preferred_element_type=jnp.float32,
    )

    def arrive(f):
        for dx in range(G):
            xs = lax.rem(x + dx, G)
            for kind in (1, 2):
                landed(slot(kind, f, xs), qkv_recv.at[kind, f, xs])
                for dc in range(1, C):
                    passed(kind, dc, f, xs).start()
        for xs in range(G):
            if f > 0:
                landed(slot(0, f, xs), qkv_recv.at[0, f, xs])
            for kind in (1, 2):
                for dc in range(1, C):
                    from_c = xs * C + lax.rem(c + C - dc, C)
                    landed(sources[kind][1].at[f, from_c], pass_recv.at[kind - 1, dc, f, xs])

    def across(r, dx):
        xx = lax.rem(x + dx, G)
        return pltpu.make_async_remote_copy(
            src_ref=ab.at[x, r, c], dst_ref=ab.at[x, r, c],
            send_sem=ax_send.at[r, dx], recv_sem=ax_recv.at[r, dx],
            **to(t, xx * C + c),
        )

    def aside(r, dx, dc):
        xs = lax.rem(x + dx, G)
        return pltpu.make_async_remote_copy(
            src_ref=ab.at[xs, r, c], dst_ref=ab.at[xs, r, c],
            send_sem=ac_send.at[r, dx, dc], recv_sem=ac_recv.at[r, dx, dc],
            **to(t, x * C + lax.rem(c + dc, C)),
        )

    scale = 1.0 / math.sqrt(HD)

    def lifted_up(r):
        return pltpu.make_async_remote_copy(
            src_ref=ab.at[x, r, c], dst_ref=ab3.at[x, r, c],
            send_sem=l_send.at[r], recv_sem=l_recv.at[r], **to(t - 1, h),
        )

    def across3(r, dx):
        xx = lax.rem(x + dx, G)
        return pltpu.make_async_remote_copy(
            src_ref=ab3.at[x, r, c], dst_ref=ab3.at[x, r, c],
            send_sem=lx_send.at[r, dx], recv_sem=lx_recv.at[r, dx],
            **to(t, xx * C + c),
        )

    def aside3(r, dx, dc):
        xs = lax.rem(x + dx, G)
        return pltpu.make_async_remote_copy(
            src_ref=ab3.at[xs, r, c], dst_ref=ab3.at[xs, r, c],
            send_sem=lc_send.at[r, dx, dc], recv_sem=lc_recv.at[r, dx, dc],
            **to(t, x * C + lax.rem(c + dc, C)),
        )

    def spread3(r):
        landed(ab3.at[x, r, c], l_recv.at[r])
        for dx in range(1, G):
            across3(r, dx).start()
        for dc in range(1, C):
            aside3(r, 0, dc).start()

    def hand_over3(r):
        for dx in range(1, G):
            xs = lax.rem(x + G - dx, G)
            landed(ab3.at[xs, r, c], lx_recv.at[r, dx])
            for dc in range(1, C):
                aside3(r, G - dx, dc).start()

    def project3(r):
        for dx in range(G):
            for dc in range(1, C):
                xs, cs = lax.rem(x + dx, G), lax.rem(c + C - dc, C)
                landed(ab3.at[xs, r, cs], lc_recv.at[r, dx, dc])
        for p in range(kept, pieces):
            cols = slice((p - kept) * nb, (p - kept + 1) * nb)
            partial = 0.0
            for xs in range(G):
                partial += jnp.dot(
                    ab3[xs, r].reshape(tokens, cw),
                    w3[xs * cw : (xs + 1) * cw, cols],
                    preferred_element_type=jnp.float32,
                )
            pb[r, p] += partial * gb[r + 1 : r + 2, p * nb : (p + 1) * nb]

    def attend(r):
        f = r + 1
        keys_here = (f + 1) * tokens
        allowed = jnp.concatenate(
            [
                jnp.broadcast_to(mb[f, mask_row + g : mask_row + g + 1, 0:1], (1, tokens))
                for g in range(f + 1)
            ],
            axis=1,
        )
        for j in range(hp):
            cols = slice(j * HD, (j + 1) * HD)
            query = qb[f, :, :, cols].reshape(half, HD)
            key = kb[0 : f + 1, :, :, cols].reshape(keys_here, HD)
            value = vb[0 : f + 1, :, :, cols].reshape(keys_here, HD)
            scores = (
                lax.dot_general(
                    query, key, (((1,), (1,)), ((), ())), preferred_element_type=jnp.float32
                )
                * scale
            )
            scores = jnp.where(allowed > 0.5, scores, -1e30)
            peak = jnp.max(scores, axis=1, keepdims=True)
            lifted = jnp.exp(scores - peak)
            total = jnp.sum(lifted, axis=1, keepdims=True)
            mixed = jnp.dot(
                lifted.astype(jnp.bfloat16), value, preferred_element_type=jnp.float32
            )
            ab[x, r, c, :, cols] = (mixed / total).astype(jnp.bfloat16)
        if r < T - 2:

            @pl.when(t == T - 1)
            def _():
                lifted_up(r).start()

        for dx in range(1, G):
            across(r, dx).start()
        for dc in range(1, C):
            aside(r, 0, dc).start()

    def down(r, p):
        return pltpu.make_async_remote_copy(
            src_ref=down_out.at[r, p], dst_ref=down_in.at[r, p],
            send_sem=dn_send.at[r, p], recv_sem=dn_recv.at[r, p], **to(t - 1, h),
        )

    def up(r, p):
        return pltpu.make_async_remote_copy(
            src_ref=up_out.at[r, p], dst_ref=up_in.at[r, p],
            send_sem=up_send.at[r, p], recv_sem=up_recv.at[r, p], **to(t + 1, h),
        )

    def hand_over(r):
        for dx in range(1, G):
            xs = lax.rem(x + G - dx, G)
            landed(ab.at[xs, r, c], ax_recv.at[r, dx])
            for dc in range(1, C):
                aside(r, G - dx, dc).start()

    def project(r):
        for dx in range(G):
            for dc in range(1, C):
                xs, cs = lax.rem(x + dx, G), lax.rem(c + C - dc, C)
                landed(ab.at[xs, r, cs], ac_recv.at[r, dx, dc])
        for p in range(pieces):
            cols = slice(p * nb, (p + 1) * nb)
            gate = gb[r + 1 : r + 2, cols]
            partial = 0.0
            for xs in range(G):
                partial += jnp.dot(
                    ab[xs, r].reshape(tokens, cw),
                    wb[xs * cw : (xs + 1) * cw, cols],
                    preferred_element_type=jnp.float32,
                )
            pb[r, p] = partial * gate

            @pl.when(t == r + 1)
            def _():
                for cs in range(C):
                    for xs in range(G):
                        rows = (cs * G + xs) * tl
                        token = (xs * C + cs) * tl
                        pb[r, p, rows : rows + tl, :] += rb[token : token + tl, cols].astype(
                            jnp.float32
                        )

            if r == T - 2 or p < kept:

                @pl.when(t == T - 1)
                def _():
                    down_out[r, p] = pb[r, p].astype(jnp.bfloat16)
                    down(r, p).start()

            if r > 0:

                @pl.when(t == 0)
                def _():
                    up_out[r, p] = pb[r, p].astype(jnp.bfloat16)
                    up(r, p).start()

    def relay_up(r):
        for p in range(pieces):

            @pl.when((t > 0) & (t < r))
            def _():
                landed(up_in.at[r, p], up_recv.at[r, p])
                up_out[r, p] = (pb[r, p] + up_in[r, p].astype(jnp.float32)).astype(jnp.bfloat16)
                up(r, p).start()

    def relay_down(r):
        for p in range(pieces):

            if p >= kept:

                @pl.when(t == T - 2)
                def _():
                    down_out[r, p] = pb[r, p].astype(jnp.bfloat16)
                    down(r, p).start()

            @pl.when((t > r) & (t < (T - 2 if p >= kept else T - 1)))
            def _():
                landed(down_in.at[r, p], dn_recv.at[r, p])
                down_out[r, p] = (pb[r, p] + down_in[r, p].astype(jnp.float32)).astype(
                    jnp.bfloat16
                )
                down(r, p).start()

    arrive(0)
    for r in range(T - 1):
        arrive(r + 1)
        attend(r)
        if r == 0:

            @pl.when(t == T - 2)
            def _():
                landed(w3.at[own_rows], w_recv.at[0])
                for dg in range(1, groups):
                    trade_weight(dg).start()

        if r > 0:
            hand_over(r - 1)
            project(r - 1)
    @pl.when(t == T - 2)
    def _():
        for r in range(T - 2):
            spread3(r)

    hand_over(T - 2)
    project(T - 2)

    @pl.when(t == T - 2)
    def _():
        for r in range(T - 2):
            hand_over3(r)
        for dg in range(1, groups):
            theirs = pl.ds(lax.rem(group + groups - dg, groups) * share, share)
            landed(w3.at[theirs], w_recv.at[dg])
        project3(0)

    relay_down(0)

    @pl.when(t == T - 2)
    def _():
        for r in range(1, T - 2):
            project3(r)

    for r in reversed(range(2, T - 1)):
        relay_up(r)
    for r in range(1, T - 2):
        relay_down(r)

    for r in range(T - 1):

        @pl.when(t == r)
        def _():
            for p in range(pieces):
                cols = slice(p * nb, (p + 1) * nb)
                landed(down_in.at[r, p], dn_recv.at[r, p])
                if r > 0:
                    landed(up_in.at[r, p], up_recv.at[r, p])
                for cs in range(C):
                    for xs in range(G):
                        rows = slice((cs * G + xs) * tl, (cs * G + xs + 1) * tl)
                        token = (xs * C + cs) * tl
                        total = pb[r, p, rows, :] + down_in[r, p, rows, :].astype(jnp.float32)
                        if r > 0:
                            total += up_in[r, p, rows, :].astype(jnp.float32)
                        out_ref[token : token + tl, cols] = total.astype(out_ref.dtype)

    @pl.when(t == T - 1)
    def _():
        copy = pltpu.make_async_copy(fresh_ref, out_ref, load_sem.at[3])
        copy.start()
        copy.wait()

    for copy in meta_copies:
        copy.wait_send()
    each_outgoing(lambda copy: copy.wait_send())

    @pl.when(t == T - 1)
    def _():
        lift_weight().wait_send()
        for r in range(T - 2):
            lifted_up(r).wait_send()

    @pl.when(t == T - 2)
    def _():
        for dg in range(1, groups):
            trade_weight(dg).wait_send()
        for r in range(T - 2):
            for dx in range(1, G):
                across3(r, dx).wait_send()
            for dx in range(G):
                for dc in range(1, C):
                    aside3(r, dx, dc).wait_send()

    for dc in range(1, C):
        for f in range(T):
            for xs in range(G):
                for kind in (1, 2):
                    passed(kind, dc, f, xs).wait_send()
    for r in range(T - 1):
        for dx in range(1, G):
            across(r, dx).wait_send()
        for dx in range(G):
            for dc in range(1, C):
                aside(r, dx, dc).wait_send()
        for p in range(pieces):

            @pl.when((t > r) if r == T - 2 or p < kept else (t > r) & (t < T - 1))
            def _():
                down(r, p).wait_send()

            @pl.when(t < r)
            def _():
                up(r, p).wait_send()


def fused(T, H, heads, groups):
    def on_device_fused(
        queries, keys, values, residual, fresh_frame, out_weight, time_weight, noise_steps, frame_mask
    ):
        level_heads = heads // T
        G = math.gcd(level_heads, H)
        C = H // G
        hp = level_heads // G
        tl = queries.shape[1]
        tokens = tl * H
        width = out_weight.shape[1]
        pieces = width // (2 * HD)
        nb = width // pieces
        kept = 2 * pieces // 5
        meta_rows = -(-(FREQ // HD + T) // 8) * 8
        meta = jnp.concatenate(
            [
                time_features(noise_steps).reshape(FREQ // HD, HD),
                jnp.broadcast_to(frame_mask[0].astype(jnp.float32)[:, None], (T, HD)),
                jnp.zeros((meta_rows - FREQ // HD - T, HD), jnp.float32),
            ],
            axis=0,
        )
        cw = hp * HD
        bf16, f32 = jnp.bfloat16, jnp.float32
        dma = pltpu.SemaphoreType.DMA
        chunk = (T - 1, pieces, tokens, nb)
        out = pl.pallas_call(
            functools.partial(fused_kernel, T, G, C, hp, pieces, kept, groups),
            out_shape=jax.ShapeDtypeStruct((tokens, width), bf16),
            in_specs=[pl.BlockSpec(memory_space=pl.ANY)] * 8,
            out_specs=pl.BlockSpec(memory_space=pltpu.VMEM),
            scratch_shapes=[
                pltpu.VMEM((T, G, tl, cw), bf16),
                pltpu.VMEM((T, H, tl, cw), bf16),
                pltpu.VMEM((T, H, tl, cw), bf16),
                pltpu.VMEM((G, T - 1, C, G * tl, cw), bf16),
                pltpu.VMEM((T, meta_rows, HD), f32),
                pltpu.VMEM((8, FREQ), f32),
                pltpu.VMEM((8, width), f32),
                pltpu.VMEM(out_weight.shape, bf16),
                pltpu.VMEM(time_weight.shape, bf16),
                pltpu.VMEM((tokens, width), bf16),
                pltpu.VMEM(chunk, f32),
                pltpu.VMEM(chunk, bf16),
                pltpu.VMEM(chunk, bf16),
                pltpu.VMEM(chunk, bf16),
                pltpu.VMEM(chunk, bf16),
                pltpu.VMEM((G, T - 1, C, G * tl, cw), bf16),
                pltpu.VMEM((level_heads * HD, (pieces - kept) * nb), bf16),
                dma((4,)),
                dma((T,)),
                dma((T,)),
                dma((3, T, G)),
                dma((3, T, G)),
                dma((2, C, T, G)),
                dma((2, C, T, G)),
                dma((T - 1, G)),
                dma((T - 1, G)),
                dma((T - 1, G, C)),
                dma((T - 1, G, C)),
                dma((T - 1, pieces)),
                dma((T - 1, pieces)),
                dma((T - 1, pieces)),
                dma((T - 1, pieces)),
                dma((groups,)),
                dma((groups,)),
                dma((T - 1,)),
                dma((T - 1,)),
                dma((T - 1, G)),
                dma((T - 1, G)),
                dma((T - 1, G, C)),
                dma((T - 1, G, C)),
            ],
            compiler_params=pltpu.CompilerParams(
                collective_id=0, has_side_effects=True, vmem_limit_bytes=56 * 1024 * 1024
            ),
        )(queries, keys, values, residual, fresh_frame, out_weight, time_weight, meta)
        return out[None]

    return on_device_fused


def solution(mesh):
    placed = (
        P(("groups", "tm"), "head", None),
        P(("groups", "tm"), "head", None),
        P(("groups", "tm"), "head", None),
        P(("groups", "tm"), None, "head"),
        P("groups", "head"),
        P("tm", "head"),
        P(None, "head"),
        P(("groups", "tm")),
        P(("groups", "tm"), None),
    )
    def whole(*args):
        frames, spread = mesh.shape["tm"], mesh.shape["head"]
        heads = args[0].shape[2] // HD
        fits = 2 < frames <= 4 and heads % frames == 0 and args[5].shape[1] % (spread * 2 * HD) == 0
        return jax.shard_map(
            fused(frames, spread, heads, mesh.shape["groups"]) if fits else on_device,
            mesh=mesh,
            in_specs=placed,
            out_specs=P(("groups", "tm"), None, "head"),
            check_vma=False,
        )(*args)

    return whole
```

profile of v0, /device:TPU:9, one launch (start us, length us, event | category | flops | bytes accessed | tf_op | source)
XLA Modules:
  0.0 85.9 jit_solution(14795520587952774983)
XLA Ops:
  0.7 0.7 convert_bitcast_fusion
  1.3 0.1 pad.1.clone
  1.4 0.1 pad.2.clone
  1.5 0.7 maximum_maximum_fusion.meta_ref
  2.2 81.7 %shard_map.91 = bf16[256,1280]{1,0:T(8,128)(2,1)} custom-call(bf16[1,64,3072]{2,1,0:T(8,128)(2,1)} %q_ref.1, bf16[1,64,3072]{2,1,0:T(8,128)(2,1)} %k_ref.1, bf16[1,64,3072]{2,1,0:T(8,128)(2,1)} %v_ref.1, bf16[1,256,1280]{2,1,0:T(8,128)(2,1)} %res_ref.1, bf16[256,1280]{1,0:T(8,128)(2,1)} %fresh_ref.1, bf16[768,1280]{1,0:T(8,128)(2,1)} %w_ref.1, ...), custom_call_target="tpu_custom_call" | custom-call | tf_op jit(solution)/shard_map/pallas_call | solution.py:594
  83.9 2.0 %copy.12 = bf16[1,256,1280]{2,1,0:T(8,128)(2,1)} copy(bf16[1,256,1280]{2,1,0:T(8,128)(2,1)} %bitcast.5) | data formatting | bytes 1310720
  (3 shorter events, 0.1 us)
where the time goes:
time: 87.3 us; the launch traced here: 85.9 us
  Pallas kernels  81.7 us (94%)
  local copies, waits for them, and re-layouts  2.12 us (2%)
  other arithmetic  1.38 us (2%)
    pallas_call x1, Pallas kernels, on_device_fused(): pl.pallas_call(functools.partial(fused_kernel, T, G, C, hp, pieces, kept,...  81.7 us
    unnamed x1, local copies, waits for them, and re-layouts  1.97 us

commit v1 on v0

v1 whole, which is shorter than its diff:
```python
import functools
import math

import jax
import jax.numpy as jnp
from jax import lax
from jax.experimental import pallas as pl
from jax.experimental.pallas import tpu as pltpu
from jax.sharding import PartitionSpec as P

HD = 128
FREQ = 256
STEPS = 50


def shifted(value, axis, steps):
    count = lax.axis_size(axis)
    leading, last = (max(0, -steps), min(count, count - steps))
    return lax.ppermute(value, axis, [(source, source + steps) for source in range(leading, last)])


def time_features(noise_steps):
    timestep = 1000.0 * (noise_steps.astype(jnp.float32) + 1.0) / STEPS
    half = FREQ // 2
    rates = jnp.exp(-math.log(10000.0) * jnp.arange(half).astype(jnp.float32) / half)
    angles = timestep[:, None] * rates[None, :]
    return jnp.concatenate([jnp.cos(angles), jnp.sin(angles)], axis=1)


def on_device(
    queries, keys, values, residual, fresh_frame, out_weight, time_weight, noise_steps, frame_mask
):
    query_local, key_local, value_local = (
        lax.all_to_all(queries, "head", split_axis=2, concat_axis=1, tiled=True),
        lax.all_to_all(keys, "head", split_axis=2, concat_axis=1, tiled=True),
        lax.all_to_all(values, "head", split_axis=2, concat_axis=1, tiled=True),
    )
    tokens = query_local.shape[1]
    heads_here = query_local.shape[2] // HD
    scale = 1.0 / math.sqrt(HD)
    query_heads = query_local[0].reshape(tokens, heads_here, HD)
    key_value = jnp.stack([key_local[0], value_local[0]], axis=0)
    frame = lax.axis_index("tm")
    frames_total = lax.axis_size("tm")
    window = min(8, frames_total)
    mask_row = frame_mask[0]
    columns = jnp.arange(mask_row.shape[0], dtype=jnp.int32)

    def allowed_at(offset):
        hits = jnp.sum(jnp.where(columns == frame - offset, mask_row, 0))
        return hits > 0

    def absorb(state, block, allowed):
        running_max, weight_sum, accumulated = state
        key_heads = block[0].reshape(tokens, heads_here, HD)
        value_heads = block[1].reshape(tokens, heads_here, HD)
        scores = (
            jnp.einsum("qhd,khd->hqk", query_heads, key_heads, preferred_element_type=jnp.float32)
            * scale
        )
        new_max = jnp.where(allowed, jnp.maximum(running_max, jnp.max(scores, axis=2)), running_max)
        lifted = jnp.where(allowed, jnp.exp(jnp.minimum(scores - new_max[:, :, None], 0.0)), 0.0)
        factor = jnp.exp(running_max - new_max)
        weight_sum = weight_sum * factor + jnp.sum(lifted, axis=2)
        rounded = lifted.astype(jnp.bfloat16)
        accumulated = accumulated * jnp.transpose(factor)[:, :, None] + jnp.einsum(
            "hqk,khd->qhd", rounded, value_heads, preferred_element_type=jnp.float32
        )
        return (new_max, weight_sum, accumulated)

    state = (
        jnp.full((heads_here, tokens), -1e30, jnp.float32),
        jnp.zeros((heads_here, tokens), jnp.float32),
        jnp.zeros((tokens, heads_here, HD), jnp.float32),
    )
    state = absorb(state, key_value, allowed_at(0))
    moving = key_value
    for offset in range(1, window):
        moving = shifted(moving, "tm", 1)
        state = absorb(state, moving, allowed_at(offset))
    running_max, weight_sum, accumulated = state
    attention = (
        (accumulated / jnp.transpose(weight_sum)[:, :, None])
        .reshape(tokens, heads_here * HD)
        .astype(jnp.bfloat16)
    )
    weight_cols = lax.all_gather(out_weight, "tm", axis=0, tiled=True)
    projected = jnp.dot(
        lax.all_gather(attention, "head", axis=1, tiled=True),
        weight_cols,
        preferred_element_type=jnp.float32,
    )
    gate = jnp.dot(
        time_features(noise_steps), time_weight.astype(jnp.float32), precision=lax.Precision.HIGHEST
    )
    updated = (residual[0].astype(jnp.float32) + gate * projected).astype(jnp.bfloat16)
    moved = shifted(updated, "tm", -1)
    rolled = jnp.where(frame == frames_total - 1, fresh_frame, moved)
    return rolled[None]


def fused_kernel(
    T, G, C, hp, pieces, groups,
    q_ref, k_ref, v_ref, res_ref, fresh_ref, w_ref, tw_ref, meta_ref,
    out_ref,
    qb, kb, vb, ab, mb, fb, gb, wb, w3, twb, rb, pb, ob, down_out, down_in, up_out, up_in,
    load_sem, out_sem, meta_send, meta_recv, qkv_send, qkv_recv, pass_send, pass_recv,
    ax_send, ax_recv, ac_send, ac_recv, dn_send, dn_recv, up_send, up_recv,
    w_send, w_recv, tr_send, tr_recv, raise_send,
):
    t = lax.axis_index("tm")
    h = lax.axis_index("head")
    group = lax.axis_index("groups")
    x = h // C
    c = lax.rem(h, C)
    H = G * C
    tl = q_ref.shape[1]
    cw = hp * HD
    tokens = tl * H
    half = G * tl
    nb = w_ref.shape[1] // pieces
    mask_row = FREQ // HD
    share = w_ref.shape[0] // groups
    top, low = T - 1, T - 2
    scale = 1.0 / math.sqrt(HD)

    def to(tt, hh):
        return dict(device_id={"tm": tt, "head": hh}, device_id_type=pl.DeviceIdType.MESH)

    def beside(dg):
        return dict(
            device_id={"groups": lax.rem(group + dg, groups)}, device_id_type=pl.DeviceIdType.MESH
        )

    def landed(ref, sem):
        pltpu.make_async_copy(ref, ref, sem).wait()

    def cols_of(p):
        return slice(p * nb, (p + 1) * nb)

    others = [(dt, dx) for dt in range(T) for dx in reversed(range(G)) if (dt, dx) != (0, 0)]

    loads = [
        pltpu.make_async_copy(tw_ref, twb, load_sem.at[0]),
        pltpu.make_async_copy(w_ref, wb, load_sem.at[1]),
        pltpu.make_async_copy(res_ref.at[0], rb, load_sem.at[2]),
    ]
    for copy in loads:
        copy.start()

    @pl.when(t == top)
    def _():
        pltpu.make_async_copy(fresh_ref, ob, load_sem.at[3]).start()

    barrier = pltpu.get_barrier_semaphore()
    for dt, dx in others:
        pl.semaphore_signal(
            barrier, inc=1, **to(lax.rem(t + dt, T), lax.rem(x + dx, G) * C + c)
        )
    for dc in range(1, C):
        pl.semaphore_signal(barrier, inc=1, **to(t, x * C + lax.rem(c + dc, C)))
    for dg in range(1, groups):
        pl.semaphore_signal(barrier, inc=1, **beside(dg))
    with jax.named_scope("barrier"):
        pl.semaphore_wait(barrier, len(others) + C - 1 + groups - 1)

    own_meta = pltpu.make_async_copy(meta_ref, mb.at[t], meta_recv.at[t])
    own_meta.start()
    meta_copies = []
    for dt in range(1, T):
        meta_copies.append(
            pltpu.make_async_remote_copy(
                src_ref=meta_ref, dst_ref=mb.at[t], send_sem=meta_send.at[dt],
                recv_sem=meta_recv.at[t], **to(lax.rem(t + dt, T), h),
            )
        )
        meta_copies[-1].start()

    sources = ((q_ref, qb), (k_ref, kb), (v_ref, vb))

    def slot(kind, s, f, xs):
        return qb.at[s, f, xs] if kind == 0 else sources[kind][1].at[s, f, xs * C + c]

    def block(kind, w, xx):
        column = pl.multiple_of((w * G + xx) * cw, HD)
        return sources[kind][0].at[0, :, pl.ds(column, cw)]

    def aim(f, key):
        w = min(key, top)
        if key < top:
            return w, 0, w
        return w, 1, (low if key == top and f < top else top)

    def outgoing(kind, f, key, dx):
        w, s, level = aim(f, key)
        xx = lax.rem(x + dx, G)
        return pltpu.make_async_remote_copy(
            src_ref=block(kind, w, xx), dst_ref=slot(kind, s, f, x),
            send_sem=qkv_send.at[kind, key, dx], recv_sem=qkv_recv.at[s, kind, f, x],
            **to(level, xx * C + c),
        )

    def own(kind, f, key):
        w, s, _ = aim(f, key)
        return pltpu.make_async_copy(
            block(kind, w, x), slot(kind, s, f, x), qkv_recv.at[s, kind, f, x]
        )

    def passed(kind, s, dc, f, xs):
        return pltpu.make_async_remote_copy(
            src_ref=slot(kind, s, f, xs), dst_ref=slot(kind, s, f, xs),
            send_sem=pass_send.at[s, kind - 1, dc, f, xs],
            recv_sem=pass_recv.at[s, kind - 1, dc, f, xs],
            **to(t, x * C + lax.rem(c + dc, C)),
        )

    def raised(kind, f, xs):
        return pltpu.make_async_remote_copy(
            src_ref=slot(kind, 1, f, xs), dst_ref=slot(kind, 1, f, xs),
            send_sem=raise_send.at[kind - 1, f, xs], recv_sem=qkv_recv.at[1, kind, f, xs],
            **to(top, h),
        )

    own_rows = pl.ds(pl.multiple_of(group * share, 8), share)

    def lift(p):
        return pltpu.make_async_remote_copy(
            src_ref=w_ref.at[own_rows, cols_of(p)], dst_ref=w3.at[own_rows, cols_of(p)],
            send_sem=w_send.at[p], recv_sem=w_recv.at[p], **to(low, h),
        )

    def trade(p, dg):
        return pltpu.make_async_remote_copy(
            src_ref=w3.at[own_rows, cols_of(p)], dst_ref=w3.at[own_rows, cols_of(p)],
            send_sem=tr_send.at[p, dg], recv_sem=tr_recv.at[p, dg], **beside(dg),
        )

    def across(s, r, dx):
        xx = lax.rem(x + dx, G)
        here = ab.at[s, r, c, :, pl.ds(pl.multiple_of(x * cw, HD), cw)]
        return pltpu.make_async_remote_copy(
            src_ref=here, dst_ref=here,
            send_sem=ax_send.at[s, r, dx], recv_sem=ax_recv.at[s, r, dx], **to(t, xx * C + c),
        )

    def aside(s, r, dx, dc):
        xs = lax.rem(x + dx, G)
        here = ab.at[s, r, c, :, pl.ds(pl.multiple_of(xs * cw, HD), cw)]
        return pltpu.make_async_remote_copy(
            src_ref=here, dst_ref=here,
            send_sem=ac_send.at[s, r, dx, dc], recv_sem=ac_recv.at[s, r, dx, dc],
            **to(t, x * C + lax.rem(c + dc, C)),
        )

    def down(level, r, p):
        return pltpu.make_async_remote_copy(
            src_ref=down_out.at[r, p], dst_ref=down_in.at[r, p],
            send_sem=dn_send.at[r, p], recv_sem=dn_recv.at[r, p], **to(level - 1, h),
        )

    def up(level, r, p):
        return pltpu.make_async_remote_copy(
            src_ref=up_out.at[r, p], dst_ref=up_in.at[r, p],
            send_sem=up_send.at[r, p], recv_sem=up_recv.at[r, p], **to(level + 1, h),
        )

    def gates():
        with jax.named_scope("loads"):
            for copy in loads:
                copy.wait()
        with jax.named_scope("meta"):
            fb[...] = jnp.zeros_like(fb)
            for f in range(T):
                landed(mb.at[f], meta_recv.at[f])
                for b in range(mask_row):
                    fb[f : f + 1, b * HD : (b + 1) * HD] = mb[f, b : b + 1, :]
        with jax.named_scope("gate"):
            gb[...] = jnp.dot(
                fb[...], twb[...].astype(jnp.float32),
                precision=lax.Precision.HIGHEST, preferred_element_type=jnp.float32,
            )

    def program(level):
        sent = []

        def send(kinds, key, dxs=tuple(reversed(range(G)))):
            for dx in dxs:
                for kind in kinds:
                    if kind == 0 and level == 0:
                        continue
                    if dx == 0 and aim(level, key)[2] == level:
                        own(kind, level, key).start()
                    else:
                        sent.append(outgoing(kind, level, key, dx))
                        sent[-1].start()

        def take(s, f, kinds=(1, 2)):
            for dx in range(G):
                xs = lax.rem(x + dx, G)
                for kind in kinds:
                    landed(slot(kind, s, f, xs), qkv_recv.at[s, kind, f, xs])
                    if kind > 0 and s == 1 and level == low and f < low:
                        sent.append(raised(kind, f, xs))
                        sent[-1].start()
                    if kind > 0:
                        for dc in range(1, C):
                            copy = passed(kind, s, dc, f, xs)
                            copy.start()
                            sent.append(copy)

        def settle(s, f):
            for xs in range(G):
                for kind in (1, 2):
                    for dc in range(1, C):
                        from_c = xs * C + lax.rem(c + C - dc, C)
                        landed(
                            sources[kind][1].at[s, f, from_c],
                            pass_recv.at[s, kind - 1, dc, f, xs],
                        )

        def attend(s, r):
            f = r + 1
            keys_here = (f + 1) * tokens
            allowed = jnp.concatenate(
                [
                    jnp.broadcast_to(mb[f, mask_row + g : mask_row + g + 1, 0:1], (1, tokens))
                    for g in range(f + 1)
                ],
                axis=1,
            )
            for j in range(hp):
                cols = slice(j * HD, (j + 1) * HD)
                query = qb[s, f, :, :, cols].reshape(half, HD)
                key = kb[s, 0 : f + 1, :, :, cols].reshape(keys_here, HD)
                value = vb[s, 0 : f + 1, :, :, cols].reshape(keys_here, HD)
                scores = (
                    lax.dot_general(
                        query, key, (((1,), (1,)), ((), ())), preferred_element_type=jnp.float32
                    )
                    * scale
                )
                scores = jnp.where(allowed > 0.5, scores, -1e30)
                peak = jnp.max(scores, axis=1, keepdims=True)
                lifted = jnp.exp(scores - peak)
                total = jnp.sum(lifted, axis=1, keepdims=True)
                mixed = jnp.dot(
                    lifted.astype(jnp.bfloat16), value, preferred_element_type=jnp.float32
                )
                place = pl.ds(pl.multiple_of(x * cw + j * HD, HD), HD)
                ab[s, r, c, :, place] = (mixed / total).astype(jnp.bfloat16)
            for dx in range(1, G):
                sent.append(across(s, r, dx))
                sent[-1].start()
            for dc in range(1, C):
                sent.append(aside(s, r, 0, dc))
                sent[-1].start()

        def hand_over(s, r):
            for dx in range(1, G):
                xs = lax.rem(x + G - dx, G)
                there = ab.at[s, r, c, :, pl.ds(pl.multiple_of(xs * cw, HD), cw)]
                landed(there, ax_recv.at[s, r, dx])
                for dc in range(1, C):
                    sent.append(aside(s, r, G - dx, dc))
                    sent[-1].start()

        def gathered(s, r):
            for dx in range(G):
                for dc in range(1, C):
                    xs, cs = lax.rem(x + dx, G), lax.rem(c + C - dc, C)
                    landed(
                        ab.at[s, r, cs, :, pl.ds(pl.multiple_of(xs * cw, HD), cw)],
                        ac_recv.at[s, r, dx, dc],
                    )

        def product(r, p):
            weights = {0: wb, 1: w3}
            if level == top:
                parts = ((1, wb),)
            elif level == low and r < low:
                parts = ((0, wb), (1, w3))
            else:
                parts = ((0, wb),)
            partial = 0.0
            for s, weight in parts:
                partial += jnp.dot(
                    ab[s, r].reshape(tokens, G * cw), weight[:, cols_of(p)],
                    preferred_element_type=jnp.float32,
                )
            partial = partial * gb[r + 1 : r + 2, cols_of(p)]
            if level == r + 1:
                moved = [
                    rb[(xs * C + cs) * tl : (xs * C + cs + 1) * tl, cols_of(p)]
                    for cs in range(C)
                    for xs in range(G)
                ]
                partial += jnp.concatenate(moved, axis=0).astype(jnp.float32)
            return partial

        def send_down(r, p, value):
            down_out[r, p] = value.astype(jnp.bfloat16)
            sent.append(down(level, r, p))
            sent[-1].start()

        def send_up(r, p, value):
            up_out[r, p] = value.astype(jnp.bfloat16)
            sent.append(up(level, r, p))
            sent[-1].start()

        def from_down(r, p):
            landed(down_in.at[r, p], dn_recv.at[r, p])
            return down_in[r, p].astype(jnp.float32)

        def from_up(r, p):
            landed(up_in.at[r, p], up_recv.at[r, p])
            return up_in[r, p].astype(jnp.float32)

        def finish(p):
            r = level
            total = pb[r, p] + from_down(r, p)
            if r > 0:
                total += from_up(r, p)
            total = total.astype(ob.dtype)
            for cs in range(C):
                for xs in range(G):
                    row, token = (cs * G + xs) * tl, (xs * C + cs) * tl
                    ob[token : token + tl, cols_of(p)] = total[row : row + tl]
            copy = pltpu.make_async_copy(
                ob.at[:, cols_of(p)], out_ref.at[:, cols_of(p)], out_sem.at[p]
            )
            copy.start()
            outs.append(copy)

        outs = []
        scope = jax.named_scope
        early = (3 * pieces) // 5
        order = [(low - 1, p) for p in range(early)]
        order += [(r, p) for r in range(low - 1) for p in range(pieces)]
        order += [(low - 1, p) for p in range(early, pieces)]
        known = set()

        if level == top:
            send((0, 1, 2), top)
            lifts = [lift(p) for p in range(pieces)]
            for p in range(early):
                lifts[p].start()
            for w in range(low):
                send((1, 2, 0), w)
            for p in range(early, pieces):
                lifts[p].start()
            send((1, 2, 0), low)
            pltpu.make_async_copy(fresh_ref, ob, load_sem.at[3]).wait()
            fresh_out = pltpu.make_async_copy(ob, out_ref, load_sem.at[3])
            fresh_out.start()
            gates()
            for f in range(T):
                with scope(f"take{f}"):
                    take(1, f)
            with scope("settle"):
                take(1, top, (0,))
                for f in range(T):
                    settle(1, f)
            with scope("attend"):
                attend(1, low)
            with scope("gather"):
                hand_over(1, low)
                gathered(1, low)
            with scope("project"):
                for p in range(pieces):
                    send_down(low, p, product(low, p))
            fresh_out.wait()
            for p in range(pieces):
                lifts[p].wait_send()
        elif level == low:
            for w in reversed(range(low)):
                send((1, 2, 0), w)
            send((1, 2, 0), low)
            send((1, 2, 0), top)
            send((1, 2), T)

            def exchange(p):
                with scope(f"trade{p}"):
                    landed(w3.at[own_rows, cols_of(p)], w_recv.at[p])
                for dg in range(1, groups):
                    sent.append(trade(p, dg))
                    sent[-1].start()

            def exchanged(p):
                for dg in range(1, groups):
                    theirs = pl.ds(
                        pl.multiple_of(lax.rem(group + groups - dg, groups) * share, 8), share
                    )
                    landed(w3.at[theirs, cols_of(p)], tr_recv.at[p, dg])

            gates()
            for p in range(early):
                exchange(p)
            for f in range(low + 1):
                for s in (0, 1):
                    with scope(f"take{f}{s}"):
                        take(s, f)
            for s in (0, 1):
                with scope(f"q{low}{s}"):
                    take(s, low, (0,))
                    for f in range(low + 1):
                        settle(s, f)
                with scope(f"attend{s}{low - 1}"):
                    attend(s, low - 1)
            for r in reversed(range(low - 1)):
                for s in (0, 1):
                    with scope(f"q{r + 1}{s}"):
                        take(s, r + 1, (0,))
                    with scope(f"attend{s}{r}"):
                        attend(s, r)
                    with scope(f"hand{s}{r + 1}"):
                        hand_over(s, r + 1)
            for s in (0, 1):
                with scope(f"hand{s}0"):
                    hand_over(s, 0)
            ready = set()
            weighed = set(range(early))
            for n, (r, p) in enumerate(order):
                if p >= early and len(weighed) < pieces:
                    for q in range(early, pieces):
                        exchange(q)
                        weighed.add(q)
                if r not in ready:
                    ready.add(r)
                    with scope(f"gather{r}"):
                        for s in (0, 1):
                            gathered(s, r)
                if p not in known:
                    known.add(p)
                    with scope(f"w{p}"):
                        exchanged(p)
                with scope(f"project{r}{p}"):
                    send_down(r, p, product(r, p))
            with scope("take3"):
                take(0, top)
                take(0, top, (0,))
                settle(0, top)
            with scope("attend3"):
                attend(0, low)
            with scope("gather3"):
                hand_over(0, low)
                gathered(0, low)
            with scope("project3"):
                for p in range(pieces):
                    pb[low, p] = product(low, p)
            for p in range(pieces):
                with scope(f"finish{p}"):
                    finish(p)
        else:
            send((1, 2), top)
            for w in range(level + 1, low + 1):
                send((1, 2), w)
            for w in range(level):
                send((1, 2, 0), w)
            for w in (top, *range(level + 1, low + 1)):
                send((0,), w)
            send((1, 2, 0), level)
            gates()
            for f in range(T - 1):
                with scope(f"take{f}"):
                    take(0, f)
                    if f > 0:
                        take(0, f, (0,))
            with scope("settle"):
                for f in range(T - 1):
                    settle(0, f)
            early = sorted(range(T - 2), key=lambda r: -r if level == 0 else r)
            for r in early:
                with scope(f"attend{r}"):
                    attend(0, r)
            for r in early:
                with scope(f"gather{r}"):
                    hand_over(0, r)
                    gathered(0, r)
                with scope(f"project{r}"):
                    for p in range(pieces):
                        value = product(r, p)
                        if level == 0 and r > 0:
                            send_up(r, p, value)
                        else:
                            pb[r, p] = value
            with scope("take3"):
                take(0, top)
                take(0, top, (0,))
                settle(0, top)
            with scope("attend3"):
                attend(0, low)
            with scope("gather3"):
                hand_over(0, low)
                gathered(0, low)
            with scope("project3"):
                for p in range(pieces):
                    value = product(low, p)
                    if level == 0:
                        send_up(low, p, value)
                    else:
                        pb[low, p] = value
            for r, p in order:
                if r > level:
                    continue
                if r == level:
                    with scope(f"finish{p}"):
                        finish(p)
                    continue
                if r == 0:
                    for q in reversed(range(level + 1, T - 1)):
                        with scope(f"up{q}{p}"):
                            send_up(q, p, pb[q, p] + from_up(q, p))
                with scope(f"down{r}{p}"):
                    send_down(r, p, pb[r, p] + from_down(r, p))
        with scope("outs"):
            for copy in outs:
                copy.wait()
        with scope("sends"):
            for copy in meta_copies:
                copy.wait_send()
            for copy in sent:
                copy.wait_send()

    for level in range(T):
        pl.when(t == level)(functools.partial(program, level))


def fused(T, H, heads, groups):
    def on_device_fused(
        queries, keys, values, residual, fresh_frame, out_weight, time_weight, noise_steps, frame_mask
    ):
        level_heads = heads // T
        G = math.gcd(level_heads, H)
        C = H // G
        hp = level_heads // G
        tl = queries.shape[1]
        tokens = tl * H
        width = out_weight.shape[1]
        pieces = width // (2 * HD)
        nb = width // pieces
        meta_rows = -(-(FREQ // HD + T) // 8) * 8
        meta = jnp.concatenate(
            [
                time_features(noise_steps).reshape(FREQ // HD, HD),
                jnp.broadcast_to(frame_mask[0].astype(jnp.float32)[:, None], (T, HD)),
                jnp.zeros((meta_rows - FREQ // HD - T, HD), jnp.float32),
            ],
            axis=0,
        )
        cw = hp * HD
        bf16, f32 = jnp.bfloat16, jnp.float32
        dma = pltpu.SemaphoreType.DMA
        chunk = (T - 1, pieces, tokens, nb)
        out = pl.pallas_call(
            functools.partial(fused_kernel, T, G, C, hp, pieces, groups),
            out_shape=jax.ShapeDtypeStruct((tokens, width), bf16),
            in_specs=[pl.BlockSpec(memory_space=pl.ANY)] * 8,
            out_specs=pl.BlockSpec(memory_space=pl.ANY),
            scratch_shapes=[
                pltpu.VMEM((2, T, G, tl, cw), bf16),
                pltpu.VMEM((2, T, H, tl, cw), bf16),
                pltpu.VMEM((2, T, H, tl, cw), bf16),
                pltpu.VMEM((2, T - 1, C, G * tl, G * cw), bf16),
                pltpu.VMEM((T, meta_rows, HD), f32),
                pltpu.VMEM((8, FREQ), f32),
                pltpu.VMEM((8, width), f32),
                pltpu.VMEM(out_weight.shape, bf16),
                pltpu.VMEM(out_weight.shape, bf16),
                pltpu.VMEM(time_weight.shape, bf16),
                pltpu.VMEM((tokens, width), bf16),
                pltpu.VMEM(chunk, f32),
                pltpu.VMEM((tokens, width), bf16),
                pltpu.VMEM(chunk, bf16),
                pltpu.VMEM(chunk, bf16),
                pltpu.VMEM(chunk, bf16),
                pltpu.VMEM(chunk, bf16),
                dma((4,)),
                dma((pieces,)),
                dma((T,)),
                dma((T,)),
                dma((3, T + 1, G)),
                dma((2, 3, T, G)),
                dma((2, 2, C, T, G)),
                dma((2, 2, C, T, G)),
                dma((2, T - 1, G)),
                dma((2, T - 1, G)),
                dma((2, T - 1, G, C)),
                dma((2, T - 1, G, C)),
                dma((T - 1, pieces)),
                dma((T - 1, pieces)),
                dma((T - 1, pieces)),
                dma((T - 1, pieces)),
                dma((pieces,)),
                dma((pieces,)),
                dma((pieces, groups)),
                dma((pieces, groups)),
                dma((2, T, G)),
            ],
            compiler_params=pltpu.CompilerParams(
                collective_id=0, has_side_effects=True, vmem_limit_bytes=56 * 1024 * 1024
            ),
        )(queries, keys, values, residual, fresh_frame, out_weight, time_weight, meta)
        return out[None]

    return on_device_fused


def solution(mesh):
    placed = (
        P(("groups", "tm"), "head", None),
        P(("groups", "tm"), "head", None),
        P(("groups", "tm"), "head", None),
        P(("groups", "tm"), None, "head"),
        P("groups", "head"),
        P("tm", "head"),
        P(None, "head"),
        P(("groups", "tm")),
        P(("groups", "tm"), None),
    )
    def whole(*args):
        frames, spread = mesh.shape["tm"], mesh.shape["head"]
        heads = args[0].shape[2] // HD
        fits = 2 < frames <= 4 and heads % frames == 0 and args[5].shape[1] % (spread * 2 * HD) == 0
        return jax.shard_map(
            fused(frames, spread, heads, mesh.shape["groups"]) if fits else on_device,
            mesh=mesh,
            in_specs=placed,
            out_specs=P(("groups", "tm"), None, "head"),
            check_vma=False,
        )(*args)

    return whole
```

time: 87.3 us -> 75.3 us (0.86)
  Pallas kernels: 81.7 us -> 70 us
    pallas_call x1, Pallas kernels: 81.7 us -> 70 us  [on_device_fused(): pl.pallas_call(functools.partial(fused_kernel, T, G, C, hp, pieces, group...]
where the time goes in v1:
time: 75.3 us; the launch traced here: 74.2 us
  Pallas kernels  70 us (93%)
  local copies, waits for them, and re-layouts  2.12 us (3%)
  other arithmetic  1.38 us (2%)
    pallas_call x1, Pallas kernels, on_device_fused(): pl.pallas_call(functools.partial(fused_kernel, T, G, C, hp, pieces, group...  70 us
    unnamed x1, local copies, waits for them, and re-layouts  1.97 us

profile of v1, /device:TPU:9, one launch (start us, length us, event | category | flops | bytes accessed | tf_op | source)
XLA Modules:
  0.0 74.2 jit_solution(1656755520376062719)
XLA Ops:
  0.7 0.7 convert_bitcast_fusion
  1.3 0.1 pad.1.clone
  1.4 0.1 pad.2.clone
  1.5 0.7 maximum_maximum_fusion.meta_ref
  2.2 70.0 %shard_map.91 = bf16[256,1280]{1,0:T(8,128)(2,1)} custom-call(bf16[1,64,3072]{2,1,0:T(8,128)(2,1)} %q_ref.1, bf16[1,64,3072]{2,1,0:T(8,128)(2,1)} %k_ref.1, bf16[1,64,3072]{2,1,0:T(8,128)(2,1)} %v_ref.1, bf16[1,256,1280]{2,1,0:T(8,128)(2,1)} %res_ref.1, bf16[256,1280]{1,0:T(8,128)(2,1)} %fresh_ref.1, bf16[768,1280]{1,0:T(8,128)(2,1)} %w_ref.1, ...), custom_call_target="tpu_custom_call" | custom-call | tf_op jit(solution)/shard_map/pallas_call | solution.py:654
  72.2 2.0 %copy.12 = bf16[1,256,1280]{2,1,0:T(8,128)(2,1)} copy(bf16[1,256,1280]{2,1,0:T(8,128)(2,1)} %bitcast.5) | data formatting | bytes 1310720
  (3 shorter events, 0.1 us)

commit v2 on v1

--- a/solution.py
+++ b/solution.py
@@ -103,10 +103,10 @@
     T, G, C, hp, pieces, groups,
     q_ref, k_ref, v_ref, res_ref, fresh_ref, w_ref, tw_ref, meta_ref,
     out_ref,
-    qb, kb, vb, ab, mb, fb, gb, wb, w3, twb, rb, pb, ob, down_out, down_in, up_out, up_in,
-    load_sem, out_sem, meta_send, meta_recv, qkv_send, qkv_recv, pass_send, pass_recv,
-    ax_send, ax_recv, ac_send, ac_recv, dn_send, dn_recv, up_send, up_recv,
-    w_send, w_recv, tr_send, tr_recv, raise_send,
+    qb, kv, ab, mb, fb, gb, wb, w3, twb, rb, pb, down_out, down_in, up_out, up_in,
+    load_sem, meta_send, meta_recv, kv_send, q_send, kv_recv, q_recv, pass_send, pass_recv,
+    raise_send, ax_send, ax_recv, ac_send, ac_recv, dn_send, dn_recv, up_send, up_recv,
+    w_send, w_recv, tr_send, tr_recv,
 ):
     t = lax.axis_index("tm")
     h = lax.axis_index("head")
@@ -150,7 +150,7 @@
 
     @pl.when(t == top)
     def _():
-        pltpu.make_async_copy(fresh_ref, ob, load_sem.at[3]).start()
+        pltpu.make_async_copy(fresh_ref, out_ref, load_sem.at[3]).start()
 
     barrier = pltpu.get_barrier_semaphore()
     for dt, dx in others:
@@ -164,26 +164,25 @@
     with jax.named_scope("barrier"):
         pl.semaphore_wait(barrier, len(others) + C - 1 + groups - 1)
 
-    own_meta = pltpu.make_async_copy(meta_ref, mb.at[t], meta_recv.at[t])
+    own_meta = pltpu.make_async_copy(meta_ref, mb.at[t], meta_recv.at[0])
     own_meta.start()
-    meta_copies = []
     for dt in range(1, T):
-        meta_copies.append(
-            pltpu.make_async_remote_copy(
-                src_ref=meta_ref, dst_ref=mb.at[t], send_sem=meta_send.at[dt],
-                recv_sem=meta_recv.at[t], **to(lax.rem(t + dt, T), h),
-            )
-        )
-        meta_copies[-1].start()
-
-    sources = ((q_ref, qb), (k_ref, kb), (v_ref, vb))
+        pltpu.make_async_remote_copy(
+            src_ref=meta_ref, dst_ref=mb.at[t], send_sem=meta_send.at[0],
+            recv_sem=meta_recv.at[0], **to(lax.rem(t + dt, T), h),
+        ).start()
+
+    sources = (q_ref, k_ref, v_ref)
 
     def slot(kind, s, f, xs):
-        return qb.at[s, f, xs] if kind == 0 else sources[kind][1].at[s, f, xs * C + c]
+        return qb.at[s * T + f, xs] if kind == 0 else kv.at[s * T + f, c, kind - 1, xs]
+
+    def sems(kind, s, f):
+        return (q_send if kind == 0 else kv_send).at[0], (q_recv if kind == 0 else kv_recv).at[s * T + f]
 
     def block(kind, w, xx):
         column = pl.multiple_of((w * G + xx) * cw, HD)
-        return sources[kind][0].at[0, :, pl.ds(column, cw)]
+        return sources[kind].at[0, :, pl.ds(column, cw)]
 
     def aim(f, key):
         w = min(key, top)
@@ -194,31 +193,27 @@
     def outgoing(kind, f, key, dx):
         w, s, level = aim(f, key)
         xx = lax.rem(x + dx, G)
+        leaves, lands = sems(kind, s, f)
         return pltpu.make_async_remote_copy(
             src_ref=block(kind, w, xx), dst_ref=slot(kind, s, f, x),
-            send_sem=qkv_send.at[kind, key, dx], recv_sem=qkv_recv.at[s, kind, f, x],
-            **to(level, xx * C + c),
+            send_sem=leaves, recv_sem=lands, **to(level, xx * C + c),
         )
 
     def own(kind, f, key):
         w, s, _ = aim(f, key)
-        return pltpu.make_async_copy(
-            block(kind, w, x), slot(kind, s, f, x), qkv_recv.at[s, kind, f, x]
-        )
-
-    def passed(kind, s, dc, f, xs):
-        return pltpu.make_async_remote_copy(
-            src_ref=slot(kind, s, f, xs), dst_ref=slot(kind, s, f, xs),
-            send_sem=pass_send.at[s, kind - 1, dc, f, xs],
-            recv_sem=pass_recv.at[s, kind - 1, dc, f, xs],
+        return pltpu.make_async_copy(block(kind, w, x), slot(kind, s, f, x), sems(kind, s, f)[1])
+
+    def passed(i, dc):
+        return pltpu.make_async_remote_copy(
+            src_ref=kv.at[i, c], dst_ref=kv.at[i, c],
+            send_sem=pass_send.at[0], recv_sem=pass_recv.at[i, dc - 1],
             **to(t, x * C + lax.rem(c + dc, C)),
         )
 
-    def raised(kind, f, xs):
-        return pltpu.make_async_remote_copy(
-            src_ref=slot(kind, 1, f, xs), dst_ref=slot(kind, 1, f, xs),
-            send_sem=raise_send.at[kind - 1, f, xs], recv_sem=qkv_recv.at[1, kind, f, xs],
-            **to(top, h),
+    def raised(i):
+        return pltpu.make_async_remote_copy(
+            src_ref=kv.at[i, c], dst_ref=kv.at[i, c],
+            send_sem=raise_send.at[0], recv_sem=kv_recv.at[i], **to(top, h),
         )
 
     own_rows = pl.ds(pl.multiple_of(group * share, 8), share)
@@ -226,42 +221,45 @@
     def lift(p):
         return pltpu.make_async_remote_copy(
             src_ref=w_ref.at[own_rows, cols_of(p)], dst_ref=w3.at[own_rows, cols_of(p)],
-            send_sem=w_send.at[p], recv_sem=w_recv.at[p], **to(low, h),
+            send_sem=w_send.at[0], recv_sem=w_recv.at[p], **to(low, h),
         )
 
     def trade(p, dg):
         return pltpu.make_async_remote_copy(
             src_ref=w3.at[own_rows, cols_of(p)], dst_ref=w3.at[own_rows, cols_of(p)],
-            send_sem=tr_send.at[p, dg], recv_sem=tr_recv.at[p, dg], **beside(dg),
-        )
-
-    def across(s, r, dx):
-        xx = lax.rem(x + dx, G)
-        here = ab.at[s, r, c, :, pl.ds(pl.multiple_of(x * cw, HD), cw)]
-        return pltpu.make_async_remote_copy(
-            src_ref=here, dst_ref=here,
-            send_sem=ax_send.at[s, r, dx], recv_sem=ax_recv.at[s, r, dx], **to(t, xx * C + c),
-        )
-
-    def aside(s, r, dx, dc):
-        xs = lax.rem(x + dx, G)
-        here = ab.at[s, r, c, :, pl.ds(pl.multiple_of(xs * cw, HD), cw)]
-        return pltpu.make_async_remote_copy(
-            src_ref=here, dst_ref=here,
-            send_sem=ac_send.at[s, r, dx, dc], recv_sem=ac_recv.at[s, r, dx, dc],
+            send_sem=tr_send.at[0], recv_sem=tr_recv.at[p, dg - 1], **beside(dg),
+        )
+
+    def mine(i, column, size):
+        return ab.at[i, c, :, pl.ds(pl.multiple_of(column, HD), size)]
+
+    def across(i, j, dx):
+        here = mine(i, x * cw + j * HD, HD)
+        return pltpu.make_async_remote_copy(
+            src_ref=here, dst_ref=here, send_sem=ax_send.at[0], recv_sem=ax_recv.at[i, dx - 1],
+            **to(t, lax.rem(x + dx, G) * C + c),
+        )
+
+    def aside(i, xs, dc):
+        here = mine(i, xs * cw, cw)
+        return pltpu.make_async_remote_copy(
+            src_ref=here, dst_ref=here, send_sem=ac_send.at[0], recv_sem=ac_recv.at[i, dc - 1],
             **to(t, x * C + lax.rem(c + dc, C)),
         )
 
+    def spot(r):
+        return r % (T - 2)
+
     def down(level, r, p):
         return pltpu.make_async_remote_copy(
-            src_ref=down_out.at[r, p], dst_ref=down_in.at[r, p],
-            send_sem=dn_send.at[r, p], recv_sem=dn_recv.at[r, p], **to(level - 1, h),
+            src_ref=down_out.at[spot(r), p], dst_ref=down_in.at[spot(r), p],
+            send_sem=dn_send.at[0], recv_sem=dn_recv.at[spot(r), p], **to(level - 1, h),
         )
 
     def up(level, r, p):
         return pltpu.make_async_remote_copy(
-            src_ref=up_out.at[r, p], dst_ref=up_in.at[r, p],
-            send_sem=up_send.at[r, p], recv_sem=up_recv.at[r, p], **to(level + 1, h),
+            src_ref=up_out.at[spot(r), p], dst_ref=up_in.at[spot(r), p],
+            send_sem=up_send.at[0], recv_sem=up_recv.at[spot(r), p], **to(level + 1, h),
         )
 
     def gates():
@@ -270,8 +268,8 @@
                 copy.wait()
         with jax.named_scope("meta"):
             fb[...] = jnp.zeros_like(fb)
+            landed(mb, meta_recv.at[0])
             for f in range(T):
-                landed(mb.at[f], meta_recv.at[f])
                 for b in range(mask_row):
                     fb[f : f + 1, b * HD : (b + 1) * HD] = mb[f, b : b + 1, :]
         with jax.named_scope("gate"):
@@ -281,7 +279,7 @@
             )
 
     def program(level):
-        sent = []
+        count = dict(kv=0, q=0, passed=0, raised=0, ax=0, ac=0, down=0, up=0, traded=0)
 
         def send(kinds, key, dxs=tuple(reversed(range(G)))):
             for dx in dxs:
@@ -291,35 +289,30 @@
                     if dx == 0 and aim(level, key)[2] == level:
                         own(kind, level, key).start()
                     else:
-                        sent.append(outgoing(kind, level, key, dx))
-                        sent[-1].start()
-
-        def take(s, f, kinds=(1, 2)):
-            for dx in range(G):
-                xs = lax.rem(x + dx, G)
-                for kind in kinds:
-                    landed(slot(kind, s, f, xs), qkv_recv.at[s, kind, f, xs])
-                    if kind > 0 and s == 1 and level == low and f < low:
-                        sent.append(raised(kind, f, xs))
-                        sent[-1].start()
-                    if kind > 0:
-                        for dc in range(1, C):
-                            copy = passed(kind, s, dc, f, xs)
-                            copy.start()
-                            sent.append(copy)
+                        outgoing(kind, level, key, dx).start()
+                        count["q" if kind == 0 else "kv"] += 1
+
+        def take(s, f):
+            i = s * T + f
+            landed(kv.at[i, c], kv_recv.at[i])
+            for dc in range(1, C):
+                passed(i, dc).start()
+                count["passed"] += 1
+            if s == 1 and level == low and f < low:
+                raised(i).start()
+                count["raised"] += 1
+
+        def take_queries(s, f):
+            landed(qb.at[s * T + f], q_recv.at[s * T + f])
 
         def settle(s, f):
-            for xs in range(G):
-                for kind in (1, 2):
-                    for dc in range(1, C):
-                        from_c = xs * C + lax.rem(c + C - dc, C)
-                        landed(
-                            sources[kind][1].at[s, f, from_c],
-                            pass_recv.at[s, kind - 1, dc, f, xs],
-                        )
+            i = s * T + f
+            for dc in range(1, C):
+                landed(kv.at[i, lax.rem(c + C - dc, C)], pass_recv.at[i, dc - 1])
 
         def attend(s, r):
             f = r + 1
+            i = s * (T - 1) + r
             keys_here = (f + 1) * tokens
             allowed = jnp.concatenate(
                 [
@@ -330,9 +323,9 @@
             )
             for j in range(hp):
                 cols = slice(j * HD, (j + 1) * HD)
-                query = qb[s, f, :, :, cols].reshape(half, HD)
-                key = kb[s, 0 : f + 1, :, :, cols].reshape(keys_here, HD)
-                value = vb[s, 0 : f + 1, :, :, cols].reshape(keys_here, HD)
+                query = qb[s * T + f, :, :, cols].reshape(half, HD)
+                key = kv[s * T : s * T + f + 1, :, 0, :, :, cols].reshape(keys_here, HD)
+                value = kv[s * T : s * T + f + 1, :, 1, :, :, cols].reshape(keys_here, HD)
                 scores = (
                     lax.dot_general(
                         query, key, (((1,), (1,)), ((), ())), preferred_element_type=jnp.float32
@@ -347,34 +340,29 @@
                     lifted.astype(jnp.bfloat16), value, preferred_element_type=jnp.float32
                 )
                 place = pl.ds(pl.multiple_of(x * cw + j * HD, HD), HD)
-                ab[s, r, c, :, place] = (mixed / total).astype(jnp.bfloat16)
-            for dx in range(1, G):
-                sent.append(across(s, r, dx))
-                sent[-1].start()
+                ab[i, c, :, place] = (mixed / total).astype(jnp.bfloat16)
+                for dx in range(1, G):
+                    across(i, j, dx).start()
+                    count["ax"] += 1
             for dc in range(1, C):
-                sent.append(aside(s, r, 0, dc))
-                sent[-1].start()
+                aside(i, x, dc).start()
+                count["ac"] += 1
 
         def hand_over(s, r):
+            i = s * (T - 1) + r
             for dx in range(1, G):
                 xs = lax.rem(x + G - dx, G)
-                there = ab.at[s, r, c, :, pl.ds(pl.multiple_of(xs * cw, HD), cw)]
-                landed(there, ax_recv.at[s, r, dx])
+                landed(mine(i, xs * cw, cw), ax_recv.at[i, dx - 1])
                 for dc in range(1, C):
-                    sent.append(aside(s, r, G - dx, dc))
-                    sent[-1].start()
+                    aside(i, xs, dc).start()
+                    count["ac"] += 1
 
         def gathered(s, r):
-            for dx in range(G):
-                for dc in range(1, C):
-                    xs, cs = lax.rem(x + dx, G), lax.rem(c + C - dc, C)
-                    landed(
-                        ab.at[s, r, cs, :, pl.ds(pl.multiple_of(xs * cw, HD), cw)],
-                        ac_recv.at[s, r, dx, dc],
-                    )
+            i = s * (T - 1) + r
+            for dc in range(1, C):
+                landed(ab.at[i, lax.rem(c + C - dc, C)], ac_recv.at[i, dc - 1])
 
         def product(r, p):
-            weights = {0: wb, 1: w3}
             if level == top:
                 parts = ((1, wb),)
             elif level == low and r < low:
@@ -384,7 +372,7 @@
             partial = 0.0
             for s, weight in parts:
                 partial += jnp.dot(
-                    ab[s, r].reshape(tokens, G * cw), weight[:, cols_of(p)],
+                    ab[s * (T - 1) + r].reshape(tokens, G * cw), weight[:, cols_of(p)],
                     preferred_element_type=jnp.float32,
                 )
             partial = partial * gb[r + 1 : r + 2, cols_of(p)]
@@ -398,46 +386,39 @@
             return partial
 
         def send_down(r, p, value):
-            down_out[r, p] = value.astype(jnp.bfloat16)
-            sent.append(down(level, r, p))
-            sent[-1].start()
+            down_out[spot(r), p] = value.astype(jnp.bfloat16)
+            down(level, r, p).start()
+            count["down"] += 1
 
         def send_up(r, p, value):
-            up_out[r, p] = value.astype(jnp.bfloat16)
-            sent.append(up(level, r, p))
-            sent[-1].start()
+            up_out[spot(r), p] = value.astype(jnp.bfloat16)
+            up(level, r, p).start()
+            count["up"] += 1
 
         def from_down(r, p):
-            landed(down_in.at[r, p], dn_recv.at[r, p])
-            return down_in[r, p].astype(jnp.float32)
+            landed(down_in.at[spot(r), p], dn_recv.at[spot(r), p])
+            return down_in[spot(r), p].astype(jnp.float32)
 
         def from_up(r, p):
-            landed(up_in.at[r, p], up_recv.at[r, p])
-            return up_in[r, p].astype(jnp.float32)
+            landed(up_in.at[spot(r), p], up_recv.at[spot(r), p])
+            return up_in[spot(r), p].astype(jnp.float32)
 
         def finish(p):
             r = level
             total = pb[r, p] + from_down(r, p)
             if r > 0:
                 total += from_up(r, p)
-            total = total.astype(ob.dtype)
+            total = total.astype(out_ref.dtype)
             for cs in range(C):
                 for xs in range(G):
                     row, token = (cs * G + xs) * tl, (xs * C + cs) * tl
-                    ob[token : token + tl, cols_of(p)] = total[row : row + tl]
-            copy = pltpu.make_async_copy(
-                ob.at[:, cols_of(p)], out_ref.at[:, cols_of(p)], out_sem.at[p]
-            )
-            copy.start()
-            outs.append(copy)
-
-        outs = []
+                    out_ref[token : token + tl, cols_of(p)] = total[row : row + tl]
+
         scope = jax.named_scope
         early = (3 * pieces) // 5
         order = [(low - 1, p) for p in range(early)]
         order += [(r, p) for r in range(low - 1) for p in range(pieces)]
         order += [(low - 1, p) for p in range(early, pieces)]
-        known = set()
 
         if level == top:
             send((0, 1, 2), top)
@@ -449,15 +430,12 @@
             for p in range(early, pieces):
                 lifts[p].start()
             send((1, 2, 0), low)
-            pltpu.make_async_copy(fresh_ref, ob, load_sem.at[3]).wait()
-            fresh_out = pltpu.make_async_copy(ob, out_ref, load_sem.at[3])
-            fresh_out.start()
             gates()
             for f in range(T):
                 with scope(f"take{f}"):
                     take(1, f)
             with scope("settle"):
-                take(1, top, (0,))
+                take_queries(1, top)
                 for f in range(T):
                     settle(1, f)
             with scope("attend"):
@@ -468,9 +446,8 @@
             with scope("project"):
                 for p in range(pieces):
                     send_down(low, p, product(low, p))
-            fresh_out.wait()
-            for p in range(pieces):
-                lifts[p].wait_send()
+            pltpu.make_async_copy(fresh_ref, out_ref, load_sem.at[3]).wait()
+            landed(w3.at[own_rows], w_send.at[0])
         elif level == low:
             for w in reversed(range(low)):
                 send((1, 2, 0), w)
@@ -482,26 +459,25 @@
                 with scope(f"trade{p}"):
                     landed(w3.at[own_rows, cols_of(p)], w_recv.at[p])
                 for dg in range(1, groups):
-                    sent.append(trade(p, dg))
-                    sent[-1].start()
+                    trade(p, dg).start()
 
             def exchanged(p):
                 for dg in range(1, groups):
                     theirs = pl.ds(
                         pl.multiple_of(lax.rem(group + groups - dg, groups) * share, 8), share
                     )
-                    landed(w3.at[theirs, cols_of(p)], tr_recv.at[p, dg])
+                    landed(w3.at[theirs, cols_of(p)], tr_recv.at[p, dg - 1])
 
             gates()
             for p in range(early):
                 exchange(p)
-            for f in range(low + 1):
+            for f in (*range(low - 1), low, low - 1):
                 for s in (0, 1):
                     with scope(f"take{f}{s}"):
                         take(s, f)
             for s in (0, 1):
                 with scope(f"q{low}{s}"):
-                    take(s, low, (0,))
+                    take_queries(s, low)
                     for f in range(low + 1):
                         settle(s, f)
                 with scope(f"attend{s}{low - 1}"):
@@ -509,38 +485,44 @@
             for r in reversed(range(low - 1)):
                 for s in (0, 1):
                     with scope(f"q{r + 1}{s}"):
-                        take(s, r + 1, (0,))
+                        take_queries(s, r + 1)
                     with scope(f"attend{s}{r}"):
                         attend(s, r)
                     with scope(f"hand{s}{r + 1}"):
                         hand_over(s, r + 1)
-            for s in (0, 1):
-                with scope(f"hand{s}0"):
-                    hand_over(s, 0)
             ready = set()
-            weighed = set(range(early))
-            for n, (r, p) in enumerate(order):
-                if p >= early and len(weighed) < pieces:
+            known = set()
+            swapped = False
+
+            def last_frame():
+                with scope("take3"):
+                    take(0, top)
+                    take_queries(0, top)
+                    settle(0, top)
+                with scope("attend3"):
+                    attend(0, low)
+
+            for r, p in order:
+                if p >= early and not swapped:
+                    swapped = True
                     for q in range(early, pieces):
                         exchange(q)
-                        weighed.add(q)
                 if r not in ready:
                     ready.add(r)
                     with scope(f"gather{r}"):
                         for s in (0, 1):
+                            if r == 0 and low > 1 or low == 1:
+                                hand_over(s, r)
+                        for s in (0, 1):
                             gathered(s, r)
                 if p not in known:
                     known.add(p)
+                    if p == pieces - 1:
+                        last_frame()
                     with scope(f"w{p}"):
                         exchanged(p)
                 with scope(f"project{r}{p}"):
                     send_down(r, p, product(r, p))
-            with scope("take3"):
-                take(0, top)
-                take(0, top, (0,))
-                settle(0, top)
-            with scope("attend3"):
-                attend(0, low)
             with scope("gather3"):
                 hand_over(0, low)
                 gathered(0, low)
@@ -550,6 +532,7 @@
             for p in range(pieces):
                 with scope(f"finish{p}"):
                     finish(p)
+            landed(w3.at[own_rows], tr_send.at[0])
         else:
             send((1, 2), top)
             for w in range(level + 1, low + 1):
@@ -564,7 +547,7 @@
                 with scope(f"take{f}"):
                     take(0, f)
                     if f > 0:
-                        take(0, f, (0,))
+                        take_queries(0, f)
             with scope("settle"):
                 for f in range(T - 1):
                     settle(0, f)
@@ -585,7 +568,7 @@
                             pb[r, p] = value
             with scope("take3"):
                 take(0, top)
-                take(0, top, (0,))
+                take_queries(0, top)
                 settle(0, top)
             with scope("attend3"):
                 attend(0, low)
@@ -612,14 +595,23 @@
                             send_up(q, p, pb[q, p] + from_up(q, p))
                 with scope(f"down{r}{p}"):
                     send_down(r, p, pb[r, p] + from_down(r, p))
-        with scope("outs"):
-            for copy in outs:
-                copy.wait()
         with scope("sends"):
-            for copy in meta_copies:
-                copy.wait_send()
-            for copy in sent:
-                copy.wait_send()
+            landed(mb.at[: T - 1], meta_send.at[0])
+            landed(kv.at[: count["kv"] // 2, 0, :, 0], kv_send.at[0])
+            if count["q"]:
+                landed(qb.at[: count["q"], 0], q_send.at[0])
+            if count["passed"]:
+                landed(kv.at[: count["passed"], 0], pass_send.at[0])
+            if count["raised"]:
+                landed(kv.at[: count["raised"], 0], raise_send.at[0])
+            if count["ax"]:
+                landed(ab.at[: count["ax"] // hp, 0, :, :cw], ax_send.at[0])
+            if count["ac"]:
+                landed(ab.at[: count["ac"] // G, 0], ac_send.at[0])
+            if count["down"]:
+                landed(down_out.at[: count["down"] // pieces], dn_send.at[0])
+            if count["up"]:
+                landed(up_out.at[: count["up"] // pieces], up_send.at[0])
 
     for level in range(T):
         pl.when(t == level)(functools.partial(program, level))
@@ -650,17 +642,17 @@
         cw = hp * HD
         bf16, f32 = jnp.bfloat16, jnp.float32
         dma = pltpu.SemaphoreType.DMA
-        chunk = (T - 1, pieces, tokens, nb)
+        chunk = (T - 2, pieces, tokens, nb)
         out = pl.pallas_call(
             functools.partial(fused_kernel, T, G, C, hp, pieces, groups),
             out_shape=jax.ShapeDtypeStruct((tokens, width), bf16),
-            in_specs=[pl.BlockSpec(memory_space=pl.ANY)] * 8,
-            out_specs=pl.BlockSpec(memory_space=pl.ANY),
+            in_specs=[pl.BlockSpec(memory_space=pltpu.HBM)] * 7
+            + [pl.BlockSpec(memory_space=pl.ANY)],
+            out_specs=pl.BlockSpec(memory_space=pltpu.VMEM),
             scratch_shapes=[
-                pltpu.VMEM((2, T, G, tl, cw), bf16),
-                pltpu.VMEM((2, T, H, tl, cw), bf16),
-                pltpu.VMEM((2, T, H, tl, cw), bf16),
-                pltpu.VMEM((2, T - 1, C, G * tl, G * cw), bf16),
+                pltpu.VMEM((2 * T, G, tl, cw), bf16),
+                pltpu.VMEM((2 * T, C, 2, G, tl, cw), bf16),
+                pltpu.VMEM((2 * (T - 1), C, G * tl, G * cw), bf16),
                 pltpu.VMEM((T, meta_rows, HD), f32),
                 pltpu.VMEM((8, FREQ), f32),
                 pltpu.VMEM((8, width), f32),
@@ -668,38 +660,46 @@
                 pltpu.VMEM(out_weight.shape, bf16),
                 pltpu.VMEM(time_weight.shape, bf16),
                 pltpu.VMEM((tokens, width), bf16),
-                pltpu.VMEM(chunk, f32),
-                pltpu.VMEM((tokens, width), bf16),
+                pltpu.VMEM((T - 1, pieces, tokens, nb), f32),
                 pltpu.VMEM(chunk, bf16),
                 pltpu.VMEM(chunk, bf16),
                 pltpu.VMEM(chunk, bf16),
                 pltpu.VMEM(chunk, bf16),
                 dma((4,)),
+                dma((1,)),
+                dma((1,)),
+                dma((1,)),
+                dma((1,)),
+                dma((2 * T,)),
+                dma((2 * T,)),
+                dma((1,)),
+                dma((2 * T, C - 1)),
+                dma((1,)),
+                dma((1,)),
+                dma((2 * (T - 1), G - 1)),
+                dma((1,)),
+                dma((2 * (T - 1), C - 1)),
+                dma((1,)),
+                dma((T - 2, pieces)),
+                dma((1,)),
+                dma((T - 2, pieces)),
+                dma((1,)),
                 dma((pieces,)),
-                dma((T,)),
-                dma((T,)),
-                dma((3, T + 1, G)),
-                dma((2, 3, T, G)),
-                dma((2, 2, C, T, G)),
-                dma((2, 2, C, T, G)),
-                dma((2, T - 1, G)),
-                dma((2, T - 1, G)),
-                dma((2, T - 1, G, C)),
-                dma((2, T - 1, G, C)),
-                dma((T - 1, pieces)),
-                dma((T - 1, pieces)),
-                dma((T - 1, pieces)),
-                dma((T - 1, pieces)),
-                dma((pieces,)),
-                dma((pieces,)),
-                dma((pieces, groups)),
-                dma((pieces, groups)),
-                dma((2, T, G)),
+                dma((1,)),
+                dma((pieces, groups - 1)),
             ],
             compiler_params=pltpu.CompilerParams(
-                collective_id=0, has_side_effects=True, vmem_limit_bytes=56 * 1024 * 1024
+                collective_id=0, has_side_effects=True, vmem_limit_bytes=32 * 1024 * 1024
             ),
-        )(queries, keys, values, residual, fresh_frame, out_weight, time_weight, meta)
+        )(
+            *(
+                pltpu.with_memory_space_constraint(array, pltpu.HBM)
+                for array in (
+                    queries, keys, values, residual, fresh_frame, out_weight, time_weight
+                )
+            ),
+            meta,
+        )
         return out[None]
 
     return on_device_fused

time: 75.3 us -> 66.8 us (0.89)
  the two profiles are of different devices: /device:TPU:9 before, /device:TPU:0 now
where the time goes in v2:
time: 66.8 us; the launch traced here: 66.6 us
  Pallas kernels  64.1 us (96%)
  local copies, waits for them, and re-layouts  0.99 us (1%)
  other arithmetic  0.78 us (1%)
  between operations  0.68 us (1%)
    pallas_call x1, Pallas kernels, on_device_fused(): pl.pallas_call(functools.partial(fused_kernel, T, G, C, hp, pieces, group...  64.1 us

profile of v2, /device:TPU:0, one launch (start us, length us, event | category | flops | bytes accessed | tf_op | source)
XLA Modules:
  0.0 66.6 jit_solution(12378791256718044833)
XLA Ops:
  0.7 0.7 convert_bitcast_fusion
  1.3 0.1 pad.1.clone
  1.4 0.1 pad.2.clone
  1.5 0.1 maximum_maximum_fusion.meta_ref
  1.6 64.1 %shard_map.91 = bf16[256,1280]{1,0:T(8,128)(2,1)S(1)} custom-call(bf16[1,64,3072]{2,1,0:T(8,128)(2,1)} %q_ref.1, bf16[1,64,3072]{2,1,0:T(8,128)(2,1)} %k_ref.1, bf16[1,64,3072]{2,1,0:T(8,128)(2,1)} %v_ref.1, bf16[1,256,1280]{2,1,0:T(8,128)(2,1)} %res_ref.1, bf16[256,1280]{1,0:T(8,128)(2,1)} %fresh_ref.1, bf16[768,1280]{1,0:T(8,128)(2,1)} %w_ref.1, ...), custom_call_target="tpu_custom_call" | custom-call | tf_op jit(solution)/shard_map/pallas_call | solution.py:646
  65.8 0.8 %copy.12 = bf16[1,256,1280]{2,1,0:T(8,128)(2,1)} copy(bf16[1,256,1280]{2,1,0:T(8,128)(2,1)S(1)} %bitcast.5) | data formatting | bytes 1310720
  (3 shorter events, 0.1 us)

commit v3 on v2

--- a/solution.py
+++ b/solution.py
@@ -101,9 +101,9 @@
 
 def fused_kernel(
     T, G, C, hp, pieces, groups,
-    q_ref, k_ref, v_ref, res_ref, fresh_ref, w_ref, tw_ref, meta_ref,
+    q_ref, k_ref, v_ref, res_ref, fresh_ref, w_ref, tw_ref, steps_ref, mask_ref,
     out_ref,
-    qb, kv, ab, mb, fb, gb, wb, w3, twb, rb, pb, down_out, down_in, up_out, up_in,
+    qb, kv, ab, lb, tb, mb, fb, gb, wb, w3, twb, rb, pb, down_out, down_in, up_out, up_in,
     load_sem, meta_send, meta_recv, kv_send, q_send, kv_recv, q_recv, pass_send, pass_recv,
     raise_send, ax_send, ax_recv, ac_send, ac_recv, dn_send, dn_recv, up_send, up_recv,
     w_send, w_recv, tr_send, tr_recv,
@@ -138,7 +138,32 @@
     def cols_of(p):
         return slice(p * nb, (p + 1) * nb)
 
-    others = [(dt, dx) for dt in range(T) for dx in reversed(range(G)) if (dt, dx) != (0, 0)]
+    def reaches(one, other):
+        return one == other or (other < top or one == low)
+
+    barrier = pltpu.get_barrier_semaphore()
+
+    def entered(level):
+        awaited = C - 1 + (groups - 1 if level == low else 0)
+        for other in range(T):
+            awaited += (G - 1 if other == level else G) * reaches(level, other)
+        return awaited
+
+    def announce(level):
+        for other in reversed(range(T)):
+            for dx in range(1 if other == level else 0, G):
+                if reaches(other, level):
+                    pl.semaphore_signal(
+                        barrier, inc=1, **to(other, lax.rem(x + dx, G) * C + c)
+                    )
+        for dc in range(1, C):
+            pl.semaphore_signal(barrier, inc=1, **to(level, x * C + lax.rem(c + dc, C)))
+        if level == low:
+            for dg in range(1, groups):
+                pl.semaphore_signal(barrier, inc=1, **beside(dg))
+
+    for level in range(T):
+        pl.when(t == level)(functools.partial(announce, level))
 
     loads = [
         pltpu.make_async_copy(tw_ref, twb, load_sem.at[0]),
@@ -152,25 +177,14 @@
     def _():
         pltpu.make_async_copy(fresh_ref, out_ref, load_sem.at[3]).start()
 
-    barrier = pltpu.get_barrier_semaphore()
-    for dt, dx in others:
-        pl.semaphore_signal(
-            barrier, inc=1, **to(lax.rem(t + dt, T), lax.rem(x + dx, G) * C + c)
-        )
-    for dc in range(1, C):
-        pl.semaphore_signal(barrier, inc=1, **to(t, x * C + lax.rem(c + dc, C)))
-    for dg in range(1, groups):
-        pl.semaphore_signal(barrier, inc=1, **beside(dg))
-    with jax.named_scope("barrier"):
-        pl.semaphore_wait(barrier, len(others) + C - 1 + groups - 1)
-
-    own_meta = pltpu.make_async_copy(meta_ref, mb.at[t], meta_recv.at[0])
-    own_meta.start()
-    for dt in range(1, T):
-        pltpu.make_async_remote_copy(
-            src_ref=meta_ref, dst_ref=mb.at[t], send_sem=meta_send.at[0],
-            recv_sem=meta_recv.at[0], **to(lax.rem(t + dt, T), h),
-        ).start()
+    timestep = 1000.0 * (jnp.full((1, HD), steps_ref[0], jnp.int32).astype(jnp.float32) + 1.0) / STEPS
+    place = lax.broadcasted_iota(jnp.int32, (1, HD), 1).astype(jnp.float32)
+    angles = timestep * jnp.exp(-math.log(10000.0) * place / (FREQ // 2))
+    mb[t, 0:1, :] = jnp.cos(angles)
+    mb[t, 1:2, :] = jnp.sin(angles)
+    for g in range(T):
+        row = mask_row + g
+        mb[t, row : row + 1, :] = jnp.full((1, HD), mask_ref[0, g], jnp.int32).astype(jnp.float32)
 
     sources = (q_ref, k_ref, v_ref)
 
@@ -178,7 +192,9 @@
         return qb.at[s * T + f, xs] if kind == 0 else kv.at[s * T + f, c, kind - 1, xs]
 
     def sems(kind, s, f):
-        return (q_send if kind == 0 else kv_send).at[0], (q_recv if kind == 0 else kv_recv).at[s * T + f]
+        if kind == 0:
+            return q_send.at[0], q_recv.at[s * T + f]
+        return kv_send.at[0], kv_recv.at[kind - 1, s * T + f]
 
     def block(kind, w, xx):
         column = pl.multiple_of((w * G + xx) * cw, HD)
@@ -203,17 +219,17 @@
         w, s, _ = aim(f, key)
         return pltpu.make_async_copy(block(kind, w, x), slot(kind, s, f, x), sems(kind, s, f)[1])
 
-    def passed(i, dc):
-        return pltpu.make_async_remote_copy(
-            src_ref=kv.at[i, c], dst_ref=kv.at[i, c],
-            send_sem=pass_send.at[0], recv_sem=pass_recv.at[i, dc - 1],
+    def passed(i, kind, dc):
+        return pltpu.make_async_remote_copy(
+            src_ref=kv.at[i, c, kind - 1], dst_ref=kv.at[i, c, kind - 1],
+            send_sem=pass_send.at[0], recv_sem=pass_recv.at[kind - 1, i, dc - 1],
             **to(t, x * C + lax.rem(c + dc, C)),
         )
 
-    def raised(i):
-        return pltpu.make_async_remote_copy(
-            src_ref=kv.at[i, c], dst_ref=kv.at[i, c],
-            send_sem=raise_send.at[0], recv_sem=kv_recv.at[i], **to(top, h),
+    def raised(i, kind):
+        return pltpu.make_async_remote_copy(
+            src_ref=kv.at[i, c, kind - 1], dst_ref=kv.at[i, c, kind - 1],
+            send_sem=raise_send.at[0], recv_sem=kv_recv.at[kind - 1, i], **to(top, h),
         )
 
     own_rows = pl.ds(pl.multiple_of(group * share, 8), share)
@@ -233,8 +249,8 @@
     def mine(i, column, size):
         return ab.at[i, c, :, pl.ds(pl.multiple_of(column, HD), size)]
 
-    def across(i, j, dx):
-        here = mine(i, x * cw + j * HD, HD)
+    def across(i, dx):
+        here = mine(i, x * cw, cw)
         return pltpu.make_async_remote_copy(
             src_ref=here, dst_ref=here, send_sem=ax_send.at[0], recv_sem=ax_recv.at[i, dx - 1],
             **to(t, lax.rem(x + dx, G) * C + c),
@@ -262,14 +278,16 @@
             send_sem=up_send.at[0], recv_sem=up_recv.at[spot(r), p], **to(level + 1, h),
         )
 
-    def gates():
+    def gates(level):
         with jax.named_scope("loads"):
             for copy in loads:
                 copy.wait()
         with jax.named_scope("meta"):
             fb[...] = jnp.zeros_like(fb)
-            landed(mb, meta_recv.at[0])
-            for f in range(T):
+            away = [f for f in range(1, T) if level != f and level < top]
+            if away:
+                landed(mb.at[: len(away)], meta_recv.at[0])
+            for f in range(1, T) if level < top else (top,):
                 for b in range(mask_row):
                     fb[f : f + 1, b * HD : (b + 1) * HD] = mb[f, b : b + 1, :]
         with jax.named_scope("gate"):
@@ -279,6 +297,15 @@
             )
 
     def program(level):
+        with jax.named_scope("barrier"):
+            pl.semaphore_wait(barrier, entered(level))
+
+        told = [other for other in range(top) if other != level and level > 0]
+        for other in told:
+            pltpu.make_async_remote_copy(
+                src_ref=mb.at[t], dst_ref=mb.at[t], send_sem=meta_send.at[0],
+                recv_sem=meta_recv.at[0], **to(other, h),
+            ).start()
         count = dict(kv=0, q=0, passed=0, raised=0, ax=0, ac=0, down=0, up=0, traded=0)
 
         def send(kinds, key, dxs=tuple(reversed(range(G)))):
@@ -292,27 +319,31 @@
                         outgoing(kind, level, key, dx).start()
                         count["q" if kind == 0 else "kv"] += 1
 
-        def take(s, f):
+        def take(s, f, kinds=(1, 2)):
             i = s * T + f
-            landed(kv.at[i, c], kv_recv.at[i])
-            for dc in range(1, C):
-                passed(i, dc).start()
-                count["passed"] += 1
-            if s == 1 and level == low and f < low:
-                raised(i).start()
-                count["raised"] += 1
+            for kind in kinds:
+                landed(kv.at[i, c, kind - 1], kv_recv.at[kind - 1, i])
+                for dc in range(1, C):
+                    passed(i, kind, dc).start()
+                    count["passed"] += 1
+                if s == 1 and level == low and f < low:
+                    raised(i, kind).start()
+                    count["raised"] += 1
 
         def take_queries(s, f):
             landed(qb.at[s * T + f], q_recv.at[s * T + f])
 
-        def settle(s, f):
+        def settle(s, f, kinds=(1, 2)):
             i = s * T + f
-            for dc in range(1, C):
-                landed(kv.at[i, lax.rem(c + C - dc, C)], pass_recv.at[i, dc - 1])
-
-        def attend(s, r):
+            for kind in kinds:
+                for dc in range(1, C):
+                    landed(
+                        kv.at[i, lax.rem(c + C - dc, C), kind - 1],
+                        pass_recv.at[kind - 1, i, dc - 1],
+                    )
+
+        def weigh(s, r, j):
             f = r + 1
-            i = s * (T - 1) + r
             keys_here = (f + 1) * tokens
             allowed = jnp.concatenate(
                 [
@@ -321,32 +352,52 @@
                 ],
                 axis=1,
             )
-            for j in range(hp):
-                cols = slice(j * HD, (j + 1) * HD)
-                query = qb[s * T + f, :, :, cols].reshape(half, HD)
-                key = kv[s * T : s * T + f + 1, :, 0, :, :, cols].reshape(keys_here, HD)
-                value = kv[s * T : s * T + f + 1, :, 1, :, :, cols].reshape(keys_here, HD)
-                scores = (
-                    lax.dot_general(
-                        query, key, (((1,), (1,)), ((), ())), preferred_element_type=jnp.float32
-                    )
-                    * scale
+            cols = slice(j * HD, (j + 1) * HD)
+            query = qb[s * T + f, :, :, cols].reshape(half, HD)
+            key = kv[s * T : s * T + f + 1, :, 0, :, :, cols].reshape(keys_here, HD)
+            scores = (
+                lax.dot_general(
+                    query, key, (((1,), (1,)), ((), ())), preferred_element_type=jnp.float32
                 )
-                scores = jnp.where(allowed > 0.5, scores, -1e30)
-                peak = jnp.max(scores, axis=1, keepdims=True)
-                lifted = jnp.exp(scores - peak)
-                total = jnp.sum(lifted, axis=1, keepdims=True)
-                mixed = jnp.dot(
-                    lifted.astype(jnp.bfloat16), value, preferred_element_type=jnp.float32
-                )
-                place = pl.ds(pl.multiple_of(x * cw + j * HD, HD), HD)
-                ab[i, c, :, place] = (mixed / total).astype(jnp.bfloat16)
-                for dx in range(1, G):
-                    across(i, j, dx).start()
-                    count["ax"] += 1
+                * scale
+            )
+            scores = jnp.where(allowed > 0.5, scores, -1e30)
+            peak = jnp.max(scores, axis=1, keepdims=True)
+            lifted = jnp.exp(scores - peak)
+            return lifted.astype(jnp.bfloat16), jnp.sum(lifted, axis=1, keepdims=True)
+
+        def mix(s, r, j, rounded, total):
+            f = r + 1
+            cols = slice(j * HD, (j + 1) * HD)
+            value = kv[s * T : s * T + f + 1, :, 1, :, :, cols].reshape((f + 1) * tokens, HD)
+            mixed = jnp.dot(rounded, value, preferred_element_type=jnp.float32)
+            here = pl.ds(pl.multiple_of(x * cw + j * HD, HD), HD)
+            ab[s * (T - 1) + r, c, :, here] = (mixed / total).astype(jnp.bfloat16)
+
+        def share_out(s, r):
+            i = s * (T - 1) + r
+            for dx in range(1, G):
+                across(i, dx).start()
+                count["ax"] += 1
             for dc in range(1, C):
                 aside(i, x, dc).start()
                 count["ac"] += 1
+
+        def attend(s, r):
+            for j in range(hp):
+                mix(s, r, j, *weigh(s, r, j))
+            share_out(s, r)
+
+        def attend_keys(s, r):
+            for j in range(hp):
+                rounded, total = weigh(s, r, j)
+                lb[s, j] = rounded
+                tb[s, j] = jnp.broadcast_to(total, (half, HD))
+
+        def attend_values(s, r):
+            for j in range(hp):
+                mix(s, r, j, lb[s, j], tb[s, j])
+            share_out(s, r)
 
         def hand_over(s, r):
             i = s * (T - 1) + r
@@ -416,21 +467,21 @@
 
         scope = jax.named_scope
         early = (3 * pieces) // 5
-        order = [(low - 1, p) for p in range(early)]
+        order = [(low - 1, p) for p in range(2)]
         order += [(r, p) for r in range(low - 1) for p in range(pieces)]
-        order += [(low - 1, p) for p in range(early, pieces)]
+        order += [(low - 1, p) for p in range(2, pieces)]
 
         if level == top:
             send((0, 1, 2), top)
             lifts = [lift(p) for p in range(pieces)]
             for p in range(early):
                 lifts[p].start()
-            for w in range(low):
+            for w in reversed(range(low)):
                 send((1, 2, 0), w)
             for p in range(early, pieces):
                 lifts[p].start()
             send((1, 2, 0), low)
-            gates()
+            gates(level)
             for f in range(T):
                 with scope(f"take{f}"):
                     take(1, f)
@@ -449,7 +500,7 @@
             pltpu.make_async_copy(fresh_ref, out_ref, load_sem.at[3]).wait()
             landed(w3.at[own_rows], w_send.at[0])
         elif level == low:
-            for w in reversed(range(low)):
+            for w in range(low):
                 send((1, 2, 0), w)
             send((1, 2, 0), low)
             send((1, 2, 0), top)
@@ -468,28 +519,41 @@
                     )
                     landed(w3.at[theirs, cols_of(p)], tr_recv.at[p, dg - 1])
 
-            gates()
-            for p in range(early):
+            gates(level)
+            for p in range(early - 1):
                 exchange(p)
-            for f in (*range(low - 1), low, low - 1):
+            with scope("take_early"):
+                for f in (*range(low - 1), low):
+                    for s in (0, 1):
+                        take(s, f)
                 for s in (0, 1):
-                    with scope(f"take{f}{s}"):
-                        take(s, f)
+                    take_queries(s, low)
+            exchange(early - 1)
+            with scope("keys"):
+                for s in (0, 1):
+                    take(s, low - 1, (1,))
             for s in (0, 1):
-                with scope(f"q{low}{s}"):
-                    take_queries(s, low)
+                with scope(f"settle{s}1"):
                     for f in range(low + 1):
-                        settle(s, f)
-                with scope(f"attend{s}{low - 1}"):
-                    attend(s, low - 1)
+                        settle(s, f, (1,))
+                with scope(f"attend{s}{low - 1}1"):
+                    attend_keys(s, low - 1)
+            for s in (0, 1):
+                with scope(f"values{s}"):
+                    take(s, low - 1, (2,))
+                with scope(f"settle{s}2"):
+                    for f in range(low + 1):
+                        settle(s, f, (2,))
+                with scope(f"attend{s}{low - 1}2"):
+                    attend_values(s, low - 1)
             for r in reversed(range(low - 1)):
                 for s in (0, 1):
+                    with scope(f"hand{s}{r + 1}"):
+                        hand_over(s, r + 1)
                     with scope(f"q{r + 1}{s}"):
                         take_queries(s, r + 1)
                     with scope(f"attend{s}{r}"):
                         attend(s, r)
-                    with scope(f"hand{s}{r + 1}"):
-                        hand_over(s, r + 1)
             ready = set()
             known = set()
             swapped = False
@@ -517,12 +581,11 @@
                             gathered(s, r)
                 if p not in known:
                     known.add(p)
-                    if p == pieces - 1:
-                        last_frame()
                     with scope(f"w{p}"):
                         exchanged(p)
                 with scope(f"project{r}{p}"):
                     send_down(r, p, product(r, p))
+            last_frame()
             with scope("gather3"):
                 hand_over(0, low)
                 gathered(0, low)
@@ -534,78 +597,75 @@
                     finish(p)
             landed(w3.at[own_rows], tr_send.at[0])
         else:
-            send((1, 2), top)
-            for w in range(level + 1, low + 1):
-                send((1, 2), w)
+            for kind in (1, 2, 0):
+                for w in (low, top):
+                    send((kind,), w)
+            for w in range(level + 1, low):
+                send((1, 2, 0), w)
             for w in range(level):
                 send((1, 2, 0), w)
-            for w in (top, *range(level + 1, low + 1)):
-                send((0,), w)
             send((1, 2, 0), level)
-            gates()
-            for f in range(T - 1):
-                with scope(f"take{f}"):
-                    take(0, f)
-                    if f > 0:
-                        take_queries(0, f)
-            with scope("settle"):
-                for f in range(T - 1):
-                    settle(0, f)
-            early = sorted(range(T - 2), key=lambda r: -r if level == 0 else r)
-            for r in early:
-                with scope(f"attend{r}"):
-                    attend(0, r)
-            for r in early:
-                with scope(f"gather{r}"):
-                    hand_over(0, r)
-                    gathered(0, r)
-                with scope(f"project{r}"):
-                    for p in range(pieces):
-                        value = product(r, p)
-                        if level == 0 and r > 0:
-                            send_up(r, p, value)
-                        else:
-                            pb[r, p] = value
-            with scope("take3"):
-                take(0, top)
-                take_queries(0, top)
-                settle(0, top)
-            with scope("attend3"):
-                attend(0, low)
-            with scope("gather3"):
-                hand_over(0, low)
-                gathered(0, low)
-            with scope("project3"):
-                for p in range(pieces):
-                    value = product(low, p)
-                    if level == 0:
-                        send_up(low, p, value)
-                    else:
-                        pb[low, p] = value
-            for r, p in order:
-                if r > level:
-                    continue
+            gates(level)
+            stages = (
+                (range(T - 1), range(T - 3, -1, -1)),
+                (range(T - 1, T), range(T - 2, T - 1)),
+            )
+            if level > 0:
+                stages = (
+                    (range(level + 1), range(level)),
+                    (range(level + 1, T), range(level, T - 1)),
+                )
+            for frames, rounds in stages:
+                for f in frames:
+                    with scope(f"take{f}"):
+                        take(0, f)
+                        if f > 0:
+                            take_queries(0, f)
+                for f in frames:
+                    with scope(f"settle{f}"):
+                        settle(0, f)
+                for r in rounds:
+                    with scope(f"attend{r}"):
+                        attend(0, r)
+                for r in rounds:
+                    with scope(f"gather{r}"):
+                        hand_over(0, r)
+                        gathered(0, r)
+                    with scope(f"project{r}"):
+                        for p in range(pieces):
+                            value = product(r, p)
+                            if level == 0 and r > 0:
+                                send_up(r, p, value)
+                            else:
+                                pb[r, p] = value
+            ups = [
+                (q, p) for p in range(pieces) for q in reversed(range(level + 1, T - 1)) if level
+            ]
+            for n, (r, p) in enumerate(pair for pair in order if pair[0] <= level):
                 if r == level:
                     with scope(f"finish{p}"):
                         finish(p)
-                    continue
-                if r == 0:
-                    for q in reversed(range(level + 1, T - 1)):
-                        with scope(f"up{q}{p}"):
-                            send_up(q, p, pb[q, p] + from_up(q, p))
-                with scope(f"down{r}{p}"):
-                    send_down(r, p, pb[r, p] + from_down(r, p))
+                else:
+                    with scope(f"down{r}{p}"):
+                        send_down(r, p, pb[r, p] + from_down(r, p))
+                if n >= 3 and ups:
+                    q, p = ups.pop(0)
+                    with scope(f"up{q}{p}"):
+                        send_up(q, p, pb[q, p] + from_up(q, p))
+            for q, p in ups:
+                send_up(q, p, pb[q, p] + from_up(q, p))
         with scope("sends"):
-            landed(mb.at[: T - 1], meta_send.at[0])
+            if told:
+                landed(mb.at[: len(told)], meta_send.at[0])
             landed(kv.at[: count["kv"] // 2, 0, :, 0], kv_send.at[0])
             if count["q"]:
                 landed(qb.at[: count["q"], 0], q_send.at[0])
             if count["passed"]:
-                landed(kv.at[: count["passed"], 0], pass_send.at[0])
+                landed(kv.at[: count["passed"] // 2, 0], pass_send.at[0])
             if count["raised"]:
-                landed(kv.at[: count["raised"], 0], raise_send.at[0])
+                landed(kv.at[: count["raised"] // 2, 0], raise_send.at[0])
             if count["ax"]:
-                landed(ab.at[: count["ax"] // hp, 0, :, :cw], ax_send.at[0])
+                landed(ab.at[: count["ax"], 0, :, :cw], ax_send.at[0])
             if count["ac"]:
                 landed(ab.at[: count["ac"] // G, 0], ac_send.at[0])
             if count["down"]:
@@ -631,14 +691,6 @@
         pieces = width // (2 * HD)
         nb = width // pieces
         meta_rows = -(-(FREQ // HD + T) // 8) * 8
-        meta = jnp.concatenate(
-            [
-                time_features(noise_steps).reshape(FREQ // HD, HD),
-                jnp.broadcast_to(frame_mask[0].astype(jnp.float32)[:, None], (T, HD)),
-                jnp.zeros((meta_rows - FREQ // HD - T, HD), jnp.float32),
-            ],
-            axis=0,
-        )
         cw = hp * HD
         bf16, f32 = jnp.bfloat16, jnp.float32
         dma = pltpu.SemaphoreType.DMA
@@ -647,12 +699,14 @@
             functools.partial(fused_kernel, T, G, C, hp, pieces, groups),
             out_shape=jax.ShapeDtypeStruct((tokens, width), bf16),
             in_specs=[pl.BlockSpec(memory_space=pltpu.HBM)] * 7
-            + [pl.BlockSpec(memory_space=pl.ANY)],
+            + [pl.BlockSpec(memory_space=pltpu.SMEM)] * 2,
             out_specs=pl.BlockSpec(memory_space=pltpu.VMEM),
             scratch_shapes=[
                 pltpu.VMEM((2 * T, G, tl, cw), bf16),
                 pltpu.VMEM((2 * T, C, 2, G, tl, cw), bf16),
                 pltpu.VMEM((2 * (T - 1), C, G * tl, G * cw), bf16),
+                pltpu.VMEM((2, hp, G * tl, (T - 1) * tokens), bf16),
+                pltpu.VMEM((2, hp, G * tl, HD), f32),
                 pltpu.VMEM((T, meta_rows, HD), f32),
                 pltpu.VMEM((8, FREQ), f32),
                 pltpu.VMEM((8, width), f32),
@@ -670,10 +724,10 @@
                 dma((1,)),
                 dma((1,)),
                 dma((1,)),
+                dma((2, 2 * T)),
                 dma((2 * T,)),
-                dma((2 * T,)),
-                dma((1,)),
-                dma((2 * T, C - 1)),
+                dma((1,)),
+                dma((2, 2 * T, C - 1)),
                 dma((1,)),
                 dma((1,)),
                 dma((2 * (T - 1), G - 1)),
@@ -698,7 +752,8 @@
                     queries, keys, values, residual, fresh_frame, out_weight, time_weight
                 )
             ),
-            meta,
+            noise_steps,
+            frame_mask,
         )
         return out[None]
 

time: 66.8 us -> 64.5 us (0.966)
  the two profiles are of different devices: /device:TPU:0 before, /device:TPU:9 now
where the time goes in v3:
time: 64.5 us; the launch traced here: 64.3 us
  Pallas kernels  62.2 us (96%)
  local copies, waits for them, and re-layouts  1.49 us (2%)
  between operations  0.67 us (1%)
    pallas_call x1, Pallas kernels, on_device_fused(): pl.pallas_call(functools.partial(fused_kernel, T, G, C, hp, pieces, group...  62.2 us
    unnamed x3, local copies, waits for them, and re-layouts  1.49 us

profile of v3, /device:TPU:9, one launch (start us, length us, event | category | flops | bytes accessed | tf_op | source)
XLA Modules:
  0.0 64.3 jit_solution(10431017048647087428)
XLA Ops:
  0.7 0.0 copy-start
  0.7 0.6 %copy-done = s32[1,4]{1,0:T(1,128)S(1)} copy-done((s32[1,4]{1,0:T(1,128)S(1)}, s32[1,4]{1,0:T(1,128)}, u32[]{:S(2)}) %copy-start) | copy-done | bytes 40
  1.3 62.2 %shard_map.91 = bf16[256,1280]{1,0:T(8,128)(2,1)S(1)} custom-call(bf16[1,64,3072]{2,1,0:T(8,128)(2,1)} %q_ref.1, bf16[1,64,3072]{2,1,0:T(8,128)(2,1)} %k_ref.1, bf16[1,64,3072]{2,1,0:T(8,128)(2,1)} %v_ref.1, bf16[1,256,1280]{2,1,0:T(8,128)(2,1)} %res_ref.1, bf16[256,1280]{1,0:T(8,128)(2,1)} %fresh_ref.1, bf16[768,1280]{1,0:T(8,128)(2,1)} %w_ref.1, ...), custom_call_target="tpu_custom_call" | custom-call | tf_op jit(solution)/shard_map/pallas_call | solution.py:698
  63.5 0.8 %copy.12 = bf16[1,256,1280]{2,1,0:T(8,128)(2,1)} copy(bf16[1,256,1280]{2,1,0:T(8,128)(2,1)S(1)} %bitcast.1) | data formatting | bytes 1310720
Async XLA Ops:
  0.7 0.7 %copy-start = (s32[1,4]{1,0:T(1,128)S(1)}, s32[1,4]{1,0:T(1,128)}, u32[]{:S(2)}) copy-start(s32[1,4]{1,0:T(1,128)} %mask_ref.1) | copy-start | bytes 52

commit v4 on v3

--- a/solution.py
+++ b/solution.py
@@ -103,10 +103,10 @@
     T, G, C, hp, pieces, groups,
     q_ref, k_ref, v_ref, res_ref, fresh_ref, w_ref, tw_ref, steps_ref, mask_ref,
     out_ref,
-    qb, kv, ab, lb, tb, mb, fb, gb, wb, w3, twb, rb, pb, down_out, down_in, up_out, up_in,
+    qb, kv, ab, lb, tb, so, st, mb, fb, gb, wb, w3, twb, rb, pb, down_out, down_in, up_out, up_in,
     load_sem, meta_send, meta_recv, kv_send, q_send, kv_recv, q_recv, pass_send, pass_recv,
     raise_send, ax_send, ax_recv, ac_send, ac_recv, dn_send, dn_recv, up_send, up_recv,
-    w_send, w_recv, tr_send, tr_recv,
+    w_send, w_recv, tr_send, tr_recv, near_send, so_send, so_recv, st_send, st_recv,
 ):
     t = lax.axis_index("tm")
     h = lax.axis_index("head")
@@ -177,14 +177,15 @@
     def _():
         pltpu.make_async_copy(fresh_ref, out_ref, load_sem.at[3]).start()
 
-    timestep = 1000.0 * (jnp.full((1, HD), steps_ref[0], jnp.int32).astype(jnp.float32) + 1.0) / STEPS
-    place = lax.broadcasted_iota(jnp.int32, (1, HD), 1).astype(jnp.float32)
-    angles = timestep * jnp.exp(-math.log(10000.0) * place / (FREQ // 2))
-    mb[t, 0:1, :] = jnp.cos(angles)
-    mb[t, 1:2, :] = jnp.sin(angles)
-    for g in range(T):
-        row = mask_row + g
-        mb[t, row : row + 1, :] = jnp.full((1, HD), mask_ref[0, g], jnp.int32).astype(jnp.float32)
+    def features():
+        timestep = 1000.0 * (jnp.full((1, HD), steps_ref[0], jnp.int32).astype(jnp.float32) + 1.0) / STEPS
+        place = lax.broadcasted_iota(jnp.int32, (1, HD), 1).astype(jnp.float32)
+        angles = timestep * jnp.exp(-math.log(10000.0) * place / (FREQ // 2))
+        mb[t, 0:1, :] = jnp.cos(angles)
+        mb[t, 1:2, :] = jnp.sin(angles)
+        for g in range(T):
+            row = mask_row + g
+            mb[t, row : row + 1, :] = jnp.full((1, HD), mask_ref[0, g], jnp.int32).astype(jnp.float32)
 
     sources = (q_ref, k_ref, v_ref)
 
@@ -231,6 +232,39 @@
             src_ref=kv.at[i, c, kind - 1], dst_ref=kv.at[i, c, kind - 1],
             send_sem=raise_send.at[0], recv_sem=kv_recv.at[kind - 1, i], **to(top, h),
         )
+
+    def near(kind, w, dx):
+        xx = lax.rem(x + dx, G)
+        leaves, lands = sems(kind, 0, w)
+        if dx == 0:
+            return pltpu.make_async_copy(block(kind, w, x), slot(kind, 0, w, x), lands)
+        return pltpu.make_async_remote_copy(
+            src_ref=block(kind, w, xx), dst_ref=slot(kind, 0, w, x),
+            send_sem=near_send.at[0] if kind == 0 else leaves, recv_sem=lands,
+            **to(top, xx * C + c),
+        )
+
+    def sidestep(k, key, dx):
+        return pltpu.make_async_remote_copy(
+            src_ref=block(0, key, lax.rem(x + dx, G)), dst_ref=qb.at[T + k, x],
+            send_sem=near_send.at[0], recv_sem=q_recv.at[T + k],
+            **to(t, lax.rem(x + dx, G) * C + c),
+        )
+
+    def forward(k, key, f, xs):
+        return pltpu.make_async_remote_copy(
+            src_ref=qb.at[T + k, xs], dst_ref=slot(0, k, f, xs),
+            send_sem=q_send.at[0], recv_sem=q_recv.at[k * T + f], **to(low, h),
+        )
+
+    def handed(w):
+        return [
+            pltpu.make_async_remote_copy(
+                src_ref=buffer.at[w], dst_ref=buffer.at[top],
+                send_sem=leaves.at[0], recv_sem=lands.at[0], **to(w, h),
+            )
+            for buffer, leaves, lands in ((so, so_send, so_recv), (st, st_send, st_recv))
+        ]
 
     own_rows = pl.ds(pl.multiple_of(group * share, 8), share)
 
@@ -297,16 +331,21 @@
             )
 
     def program(level):
+        if level < top:
+            features()
         with jax.named_scope("barrier"):
             pl.semaphore_wait(barrier, entered(level))
-
+        if level == top:
+            lifts = [lift(p) for p in range(pieces)]
+            lifts[0].start()
+            features()
         told = [other for other in range(top) if other != level and level > 0]
         for other in told:
             pltpu.make_async_remote_copy(
                 src_ref=mb.at[t], dst_ref=mb.at[t], send_sem=meta_send.at[0],
                 recv_sem=meta_recv.at[0], **to(other, h),
             ).start()
-        count = dict(kv=0, q=0, passed=0, raised=0, ax=0, ac=0, down=0, up=0, traded=0)
+        count = dict(kv=0, q=0, passed=0, raised=0, near=0, ax=0, ac=0, down=0, up=0, traded=0)
 
         def send(kinds, key, dxs=tuple(reversed(range(G)))):
             for dx in dxs:
@@ -374,6 +413,71 @@
             here = pl.ds(pl.multiple_of(x * cw + j * HD, HD), HD)
             ab[s * (T - 1) + r, c, :, here] = (mixed / total).astype(jnp.bfloat16)
 
+        def attend_own(w):
+            lane = lax.broadcasted_iota(jnp.int32, (half, HD), 1)
+            stats = jnp.zeros((half, HD), jnp.float32)
+            for j in range(hp):
+                cols = slice(j * HD, (j + 1) * HD)
+                query = qb[w, :, :, cols].reshape(half, HD)
+                key = kv[w, :, 0, :, :, cols].reshape(tokens, HD)
+                value = kv[w, :, 1, :, :, cols].reshape(tokens, HD)
+                scores = (
+                    lax.dot_general(
+                        query, key, (((1,), (1,)), ((), ())), preferred_element_type=jnp.float32
+                    )
+                    * scale
+                )
+                peak = jnp.max(scores, axis=1, keepdims=True)
+                lifted = jnp.exp(scores - peak)
+                total = jnp.sum(lifted, axis=1, keepdims=True)
+                mixed = jnp.dot(
+                    lifted.astype(jnp.bfloat16), value, preferred_element_type=jnp.float32
+                )
+                so[w, :, cols] = (mixed / total).astype(jnp.bfloat16)
+                stats = jnp.where(lane == 2 * j, peak, stats)
+                stats = jnp.where(lane == 2 * j + 1, total, stats)
+            st[w] = jnp.transpose(stats)[:8]
+            for copy in handed(w):
+                copy.start()
+
+        def attend_last():
+            landed(so.at[top], so_recv.at[0])
+            landed(st.at[top], st_recv.at[0])
+            stats = jnp.transpose(
+                jnp.concatenate([st[top], jnp.zeros((HD - 8, half), jnp.float32)], axis=0)
+            )
+            allowed = jnp.concatenate(
+                [
+                    jnp.broadcast_to(mb[top, mask_row + g : mask_row + g + 1, 0:1], (1, tokens))
+                    for g in range(top)
+                ],
+                axis=1,
+            )
+            for j in range(hp):
+                cols = slice(j * HD, (j + 1) * HD)
+                query = qb[top, :, :, cols].reshape(half, HD)
+                key = kv[0:top, :, 0, :, :, cols].reshape(top * tokens, HD)
+                value = kv[0:top, :, 1, :, :, cols].reshape(top * tokens, HD)
+                scores = (
+                    lax.dot_general(
+                        query, key, (((1,), (1,)), ((), ())), preferred_element_type=jnp.float32
+                    )
+                    * scale
+                )
+                scores = jnp.where(allowed > 0.5, scores, -1e30)
+                their_peak = stats[:, 2 * j : 2 * j + 1]
+                peak = jnp.maximum(jnp.max(scores, axis=1, keepdims=True), their_peak)
+                lifted = jnp.exp(scores - peak)
+                theirs = jnp.exp(their_peak - peak) * stats[:, 2 * j + 1 : 2 * j + 2]
+                total = jnp.sum(lifted, axis=1, keepdims=True) + theirs
+                mixed = jnp.dot(
+                    lifted.astype(jnp.bfloat16), value, preferred_element_type=jnp.float32
+                )
+                mixed += theirs * so[top, :, cols].astype(jnp.float32)
+                here = pl.ds(pl.multiple_of(x * cw + j * HD, HD), HD)
+                ab[low, c, :, here] = (mixed / total).astype(jnp.bfloat16)
+            share_out(0, low)
+
         def share_out(s, r):
             i = s * (T - 1) + r
             for dx in range(1, G):
@@ -472,12 +576,26 @@
         order += [(low - 1, p) for p in range(2, pieces)]
 
         if level == top:
+            for p in range(1, early):
+                lifts[p].start()
+            lower = tuple(reversed(range(low)))
+            for w in lower:
+                for dx in reversed(range(G)):
+                    for kind in (1, 0, 2):
+                        near(kind, w, dx).start()
+                        if dx > 0:
+                            count["near" if kind == 0 else "kv"] += 1
+            for w in lower:
+                send((0,), w)
             send((0, 1, 2), top)
-            lifts = [lift(p) for p in range(pieces)]
-            for p in range(early):
-                lifts[p].start()
-            for w in reversed(range(low)):
-                send((1, 2, 0), w)
+            for w in lower:
+                with scope(f"near{w}"):
+                    take(0, w)
+                    take_queries(0, w)
+            for w in lower:
+                with scope(f"own{w}"):
+                    settle(0, w)
+                    attend_own(w)
             for p in range(early, pieces):
                 lifts[p].start()
             send((1, 2, 0), low)
@@ -528,10 +646,10 @@
                         take(s, f)
                 for s in (0, 1):
                     take_queries(s, low)
-            exchange(early - 1)
             with scope("keys"):
                 for s in (0, 1):
                     take(s, low - 1, (1,))
+            exchange(early - 1)
             for s in (0, 1):
                 with scope(f"settle{s}1"):
                     for f in range(low + 1):
@@ -569,10 +687,12 @@
             for r, p in order:
                 if p >= early and not swapped:
                     swapped = True
-                    for q in range(early, pieces):
+                    for q in range(early + 1, pieces):
                         exchange(q)
                 if r not in ready:
                     ready.add(r)
+                    if r == 0:
+                        exchange(early)
                     with scope(f"gather{r}"):
                         for s in (0, 1):
                             if r == 0 and low > 1 or low == 1:
@@ -597,15 +717,29 @@
                     finish(p)
             landed(w3.at[own_rows], tr_send.at[0])
         else:
-            for kind in (1, 2, 0):
+            if level > 0:
+                for k, w in enumerate((low, top)):
+                    for dx in range(1, G):
+                        sidestep(k, w, dx).start()
+                        count["near"] += 1
+            for kind in (1, 2):
                 for w in (low, top):
                     send((kind,), w)
+            for w in (low, top):
+                send((0,), w, (0,))
             for w in range(level + 1, low):
                 send((1, 2, 0), w)
             for w in range(level):
                 send((1, 2, 0), w)
             send((1, 2, 0), level)
             gates(level)
+            if level > 0:
+                for k, w in enumerate((low, top)):
+                    for dx in range(1, G):
+                        xs = lax.rem(x + dx, G)
+                        landed(qb.at[T + k, xs], q_recv.at[T + k])
+                        forward(k, w, level, xs).start()
+                        count["q"] += 1
             stages = (
                 (range(T - 1), range(T - 3, -1, -1)),
                 (range(T - 1, T), range(T - 2, T - 1)),
@@ -618,15 +752,20 @@
             for frames, rounds in stages:
                 for f in frames:
                     with scope(f"take{f}"):
-                        take(0, f)
+                        if f < top:
+                            take(0, f)
                         if f > 0:
                             take_queries(0, f)
                 for f in frames:
                     with scope(f"settle{f}"):
-                        settle(0, f)
+                        if f < top:
+                            settle(0, f)
                 for r in rounds:
                     with scope(f"attend{r}"):
-                        attend(0, r)
+                        if r < low:
+                            attend(0, r)
+                        else:
+                            attend_last()
                 for r in rounds:
                     with scope(f"gather{r}"):
                         hand_over(0, r)
@@ -660,6 +799,11 @@
             landed(kv.at[: count["kv"] // 2, 0, :, 0], kv_send.at[0])
             if count["q"]:
                 landed(qb.at[: count["q"], 0], q_send.at[0])
+            if count["near"]:
+                landed(qb.at[: count["near"], 0], near_send.at[0])
+            if level == top:
+                landed(so.at[:low], so_send.at[0])
+                landed(st.at[:low], st_send.at[0])
             if count["passed"]:
                 landed(kv.at[: count["passed"] // 2, 0], pass_send.at[0])
             if count["raised"]:
@@ -707,6 +851,8 @@
                 pltpu.VMEM((2 * (T - 1), C, G * tl, G * cw), bf16),
                 pltpu.VMEM((2, hp, G * tl, (T - 1) * tokens), bf16),
                 pltpu.VMEM((2, hp, G * tl, HD), f32),
+                pltpu.VMEM((T, G * tl, cw), bf16),
+                pltpu.VMEM((T, 8, G * tl), f32),
                 pltpu.VMEM((T, meta_rows, HD), f32),
                 pltpu.VMEM((8, FREQ), f32),
                 pltpu.VMEM((8, width), f32),
@@ -741,6 +887,11 @@
                 dma((pieces,)),
                 dma((1,)),
                 dma((pieces, groups - 1)),
+                dma((1,)),
+                dma((1,)),
+                dma((1,)),
+                dma((1,)),
+                dma((1,)),
             ],
             compiler_params=pltpu.CompilerParams(
                 collective_id=0, has_side_effects=True, vmem_limit_bytes=32 * 1024 * 1024

time: 64.5 us -> 63.3 us (0.981)
  Pallas kernels: 62.2 us -> 61 us
    pallas_call x1, Pallas kernels: 62.2 us -> 61 us  [on_device_fused(): pl.pallas_call(functools.partial(fused_kernel, T, G, C, hp, pieces, group...]
where the time goes in v4:
time: 63.3 us; the launch traced here: 63.1 us
  Pallas kernels  61 us (96%)
  local copies, waits for them, and re-layouts  1.49 us (2%)
  between operations  0.67 us (1%)
    pallas_call x1, Pallas kernels, on_device_fused(): pl.pallas_call(functools.partial(fused_kernel, T, G, C, hp, pieces, group...  61 us
    unnamed x3, local copies, waits for them, and re-layouts  1.49 us

profile of v4, /device:TPU:9, one launch (start us, length us, event | category | flops | bytes accessed | tf_op | source)
XLA Modules:
  0.0 63.1 jit_solution(8657842976707241215)
XLA Ops:
  0.7 0.0 copy-start
  0.7 0.6 %copy-done = s32[1,4]{1,0:T(1,128)S(1)} copy-done((s32[1,4]{1,0:T(1,128)S(1)}, s32[1,4]{1,0:T(1,128)}, u32[]{:S(2)}) %copy-start) | copy-done | bytes 40
  1.3 61.0 %shard_map.91 = bf16[256,1280]{1,0:T(8,128)(2,1)S(1)} custom-call(bf16[1,64,3072]{2,1,0:T(8,128)(2,1)} %q_ref.1, bf16[1,64,3072]{2,1,0:T(8,128)(2,1)} %k_ref.1, bf16[1,64,3072]{2,1,0:T(8,128)(2,1)} %v_ref.1, bf16[1,256,1280]{2,1,0:T(8,128)(2,1)} %res_ref.1, bf16[256,1280]{1,0:T(8,128)(2,1)} %fresh_ref.1, bf16[768,1280]{1,0:T(8,128)(2,1)} %w_ref.1, ...), custom_call_target="tpu_custom_call" | custom-call | tf_op jit(solution)/shard_map/pallas_call | solution.py:842
  62.3 0.8 %copy.12 = bf16[1,256,1280]{2,1,0:T(8,128)(2,1)} copy(bf16[1,256,1280]{2,1,0:T(8,128)(2,1)S(1)} %bitcast.1) | data formatting | bytes 1310720
Async XLA Ops:
  0.7 0.7 %copy-start = (s32[1,4]{1,0:T(1,128)S(1)}, s32[1,4]{1,0:T(1,128)}, u32[]{:S(2)}) copy-start(s32[1,4]{1,0:T(1,128)} %mask_ref.1) | copy-start | bytes 52

commit v5 on v4

--- a/solution.py
+++ b/solution.py
@@ -539,6 +539,44 @@
                 ]
                 partial += jnp.concatenate(moved, axis=0).astype(jnp.float32)
             return partial
+
+        def part(r, p, dc, going_up):
+            cc = lax.rem(c + dc, C)
+            parts = ((0, wb), (1, w3)) if level == low and r < low else ((0, wb),)
+            partial = 0.0
+            for s, weight in parts:
+                partial += jnp.dot(
+                    ab[s * (T - 1) + r, cc], weight[:, cols_of(p)],
+                    preferred_element_type=jnp.float32,
+                )
+            partial = partial * gb[r + 1 : r + 2, cols_of(p)]
+            if level == r + 1:
+                moved = [
+                    rb[pl.ds(pl.multiple_of((xs * C + cc) * tl, tl), tl), cols_of(p)]
+                    for xs in range(G)
+                ]
+                partial += jnp.concatenate(moved, axis=0).astype(jnp.float32)
+            rows = pl.ds(pl.multiple_of(cc * half, half), half)
+            out, into = (up_out, up_in) if going_up else (down_out, down_in)
+            leaves, lands = (up_send, up_recv) if going_up else (dn_send, dn_recv)
+            out[spot(r), p, rows, :] = partial.astype(jnp.bfloat16)
+            pltpu.make_async_remote_copy(
+                src_ref=out.at[spot(r), p, rows], dst_ref=into.at[spot(r), p, rows],
+                send_sem=leaves.at[0], recv_sem=lands.at[spot(r), p],
+                **to(level + 1 if going_up else level - 1, h),
+            ).start()
+
+        def own_parts(r, going_up=False):
+            for p in range(2):
+                with scope(f"own{r}{p}"):
+                    part(r, p, 0, going_up)
+                count["up" if going_up else "down"] += 1
+
+        def other_parts(r, going_up=False):
+            for p in range(2):
+                for dc in range(1, C):
+                    with scope(f"other{r}{p}"):
+                        part(r, p, dc, going_up)
 
         def send_down(r, p, value):
             down_out[spot(r), p] = value.astype(jnp.bfloat16)
@@ -668,12 +706,16 @@
                 for s in (0, 1):
                     with scope(f"hand{s}{r + 1}"):
                         hand_over(s, r + 1)
+                    if s == 1:
+                        for p in range(2):
+                            exchanged(p)
+                        own_parts(r + 1)
                     with scope(f"q{r + 1}{s}"):
                         take_queries(s, r + 1)
                     with scope(f"attend{s}{r}"):
                         attend(s, r)
             ready = set()
-            known = set()
+            known = {0, 1} if low > 1 else set()
             swapped = False
 
             def last_frame():
@@ -693,12 +735,21 @@
                     ready.add(r)
                     if r == 0:
                         exchange(early)
+                    if r == 0:
+                        for s in (0, 1):
+                            with scope(f"hand{s}{r}"):
+                                hand_over(s, r)
+                        for q in range(2):
+                            if q not in known:
+                                known.add(q)
+                                exchanged(q)
+                        own_parts(r)
                     with scope(f"gather{r}"):
                         for s in (0, 1):
-                            if r == 0 and low > 1 or low == 1:
-                                hand_over(s, r)
-                        for s in (0, 1):
                             gathered(s, r)
+                    other_parts(r)
+                if p < 2:
+                    continue
                 if p not in known:
                     known.add(p)
                     with scope(f"w{p}"):
@@ -767,11 +818,17 @@
                         else:
                             attend_last()
                 for r in rounds:
+                    early_up = level == 0 and 0 < r < low
                     with scope(f"gather{r}"):
                         hand_over(0, r)
+                    if early_up:
+                        own_parts(r, True)
+                    with scope(f"pair{r}"):
                         gathered(0, r)
+                    if early_up:
+                        other_parts(r, True)
                     with scope(f"project{r}"):
-                        for p in range(pieces):
+                        for p in range(2 if early_up else 0, pieces):
                             value = product(r, p)
                             if level == 0 and r > 0:
                                 send_up(r, p, value)

time: 63.3 us -> 62.1 us (0.981); the launches traced: 63.1 us -> 61 us
  Pallas kernels: 61 us -> 58.8 us
    pallas_call x1, Pallas kernels: 61 us -> 58.8 us  [on_device_fused(): pl.pallas_call(functools.partial(fused_kernel, T, G, C, hp, pieces, group...]
where the time goes in v5:
time: 62.1 us; the launch traced here: 61 us
  Pallas kernels  58.8 us (95%)
  local copies, waits for them, and re-layouts  1.49 us (2%)
  between operations  0.67 us (1%)
    pallas_call x1, Pallas kernels, on_device_fused(): pl.pallas_call(functools.partial(fused_kernel, T, G, C, hp, pieces, group...  58.8 us
    unnamed x3, local copies, waits for them, and re-layouts  1.49 us

profile of v5, /device:TPU:9, one launch (start us, length us, event | category | flops | bytes accessed | tf_op | source)
XLA Modules:
  0.0 61.0 jit_solution(15494753307261019806)
XLA Ops:
  0.7 0.0 copy-start
  0.7 0.6 %copy-done = s32[1,4]{1,0:T(1,128)S(1)} copy-done((s32[1,4]{1,0:T(1,128)S(1)}, s32[1,4]{1,0:T(1,128)}, u32[]{:S(2)}) %copy-start) | copy-done | bytes 40
  1.3 58.8 %shard_map.91 = bf16[256,1280]{1,0:T(8,128)(2,1)S(1)} custom-call(bf16[1,64,3072]{2,1,0:T(8,128)(2,1)} %q_ref.1, bf16[1,64,3072]{2,1,0:T(8,128)(2,1)} %k_ref.1, bf16[1,64,3072]{2,1,0:T(8,128)(2,1)} %v_ref.1, bf16[1,256,1280]{2,1,0:T(8,128)(2,1)} %res_ref.1, bf16[256,1280]{1,0:T(8,128)(2,1)} %fresh_ref.1, bf16[768,1280]{1,0:T(8,128)(2,1)} %w_ref.1, ...), custom_call_target="tpu_custom_call" | custom-call | tf_op jit(solution)/shard_map/pallas_call | solution.py:899
  60.2 0.8 %copy.12 = bf16[1,256,1280]{2,1,0:T(8,128)(2,1)} copy(bf16[1,256,1280]{2,1,0:T(8,128)(2,1)S(1)} %bitcast.1) | data formatting | bytes 1310720
Async XLA Ops:
  0.7 0.7 %copy-start = (s32[1,4]{1,0:T(1,128)S(1)}, s32[1,4]{1,0:T(1,128)}, u32[]{:S(2)}) copy-start(s32[1,4]{1,0:T(1,128)} %mask_ref.1) | copy-start | bytes 52

commit v6 on v5

--- a/solution.py
+++ b/solution.py
@@ -106,7 +106,7 @@
     qb, kv, ab, lb, tb, so, st, mb, fb, gb, wb, w3, twb, rb, pb, down_out, down_in, up_out, up_in,
     load_sem, meta_send, meta_recv, kv_send, q_send, kv_recv, q_recv, pass_send, pass_recv,
     raise_send, ax_send, ax_recv, ac_send, ac_recv, dn_send, dn_recv, up_send, up_recv,
-    w_send, w_recv, tr_send, tr_recv, near_send, so_send, so_recv, st_send, st_recv,
+    w_send, tr_send, tr_recv, near_send, so_send, so_recv, st_send, st_recv,
 ):
     t = lax.axis_index("tm")
     h = lax.axis_index("head")
@@ -220,10 +220,10 @@
         w, s, _ = aim(f, key)
         return pltpu.make_async_copy(block(kind, w, x), slot(kind, s, f, x), sems(kind, s, f)[1])
 
-    def passed(i, kind, dc):
+    def passed(i, kind, dc, late):
         return pltpu.make_async_remote_copy(
             src_ref=kv.at[i, c, kind - 1], dst_ref=kv.at[i, c, kind - 1],
-            send_sem=pass_send.at[0], recv_sem=pass_recv.at[kind - 1, i, dc - 1],
+            send_sem=pass_send.at[0], recv_sem=pass_recv.at[kind - 1, late, dc - 1],
             **to(t, x * C + lax.rem(c + dc, C)),
         )
 
@@ -271,7 +271,7 @@
     def lift(p):
         return pltpu.make_async_remote_copy(
             src_ref=w_ref.at[own_rows, cols_of(p)], dst_ref=w3.at[own_rows, cols_of(p)],
-            send_sem=w_send.at[0], recv_sem=w_recv.at[p], **to(low, h),
+            send_sem=w_send.at[0], recv_sem=dn_recv.at[1, p], **to(low, h),
         )
 
     def trade(p, dg):
@@ -358,12 +358,19 @@
                         outgoing(kind, level, key, dx).start()
                         count["q" if kind == 0 else "kv"] += 1
 
+        def group_of(s, f):
+            if level == top:
+                return T if s else f
+            if level == low:
+                return 2 * s + (f == top)
+            return int(0 < level < f)
+
         def take(s, f, kinds=(1, 2)):
             i = s * T + f
             for kind in kinds:
                 landed(kv.at[i, c, kind - 1], kv_recv.at[kind - 1, i])
                 for dc in range(1, C):
-                    passed(i, kind, dc).start()
+                    passed(i, kind, dc, group_of(s, f)).start()
                     count["passed"] += 1
                 if s == 1 and level == low and f < low:
                     raised(i, kind).start()
@@ -372,13 +379,13 @@
         def take_queries(s, f):
             landed(qb.at[s * T + f], q_recv.at[s * T + f])
 
-        def settle(s, f, kinds=(1, 2)):
-            i = s * T + f
+        def settle(s, frames, kinds=(1, 2)):
+            i = s * T + frames[0]
             for kind in kinds:
                 for dc in range(1, C):
                     landed(
-                        kv.at[i, lax.rem(c + C - dc, C), kind - 1],
-                        pass_recv.at[kind - 1, i, dc - 1],
+                        kv.at[i : i + len(frames), lax.rem(c + C - dc, C), kind - 1],
+                        pass_recv.at[kind - 1, group_of(s, frames[0]), dc - 1],
                     )
 
         def weigh(s, r, j):
@@ -632,7 +639,7 @@
                     take_queries(0, w)
             for w in lower:
                 with scope(f"own{w}"):
-                    settle(0, w)
+                    settle(0, (w,))
                     attend_own(w)
             for p in range(early, pieces):
                 lifts[p].start()
@@ -643,8 +650,7 @@
                     take(1, f)
             with scope("settle"):
                 take_queries(1, top)
-                for f in range(T):
-                    settle(1, f)
+                settle(1, range(T))
             with scope("attend"):
                 attend(1, low)
             with scope("gather"):
@@ -664,7 +670,7 @@
 
             def exchange(p):
                 with scope(f"trade{p}"):
-                    landed(w3.at[own_rows, cols_of(p)], w_recv.at[p])
+                    landed(w3.at[own_rows, cols_of(p)], dn_recv.at[1, p])
                 for dg in range(1, groups):
                     trade(p, dg).start()
 
@@ -690,16 +696,14 @@
             exchange(early - 1)
             for s in (0, 1):
                 with scope(f"settle{s}1"):
-                    for f in range(low + 1):
-                        settle(s, f, (1,))
+                    settle(s, range(low + 1), (1,))
                 with scope(f"attend{s}{low - 1}1"):
                     attend_keys(s, low - 1)
             for s in (0, 1):
                 with scope(f"values{s}"):
                     take(s, low - 1, (2,))
                 with scope(f"settle{s}2"):
-                    for f in range(low + 1):
-                        settle(s, f, (2,))
+                    settle(s, range(low + 1), (2,))
                 with scope(f"attend{s}{low - 1}2"):
                     attend_values(s, low - 1)
             for r in reversed(range(low - 1)):
@@ -722,7 +726,7 @@
                 with scope("take3"):
                     take(0, top)
                     take_queries(0, top)
-                    settle(0, top)
+                    settle(0, (top,))
                 with scope("attend3"):
                     attend(0, low)
 
@@ -807,10 +811,8 @@
                             take(0, f)
                         if f > 0:
                             take_queries(0, f)
-                for f in frames:
-                    with scope(f"settle{f}"):
-                        if f < top:
-                            settle(0, f)
+                if frames[0] < top:
+                    settle(0, range(frames[0], min(frames[-1] + 1, top)))
                 for r in rounds:
                     with scope(f"attend{r}"):
                         if r < low:
@@ -828,12 +830,15 @@
                     if early_up:
                         other_parts(r, True)
                     with scope(f"project{r}"):
-                        for p in range(2 if early_up else 0, pieces):
+                        for p in range(2 if early_up else 0, pieces - early_up):
                             value = product(r, p)
                             if level == 0 and r > 0:
                                 send_up(r, p, value)
                             else:
                                 pb[r, p] = value
+            if level == 0:
+                for r in range(1, low):
+                    send_up(r, pieces - 1, product(r, pieces - 1))
             ups = [
                 (q, p) for p in range(pieces) for q in reversed(range(level + 1, T - 1)) if level
             ]
@@ -844,7 +849,7 @@
                 else:
                     with scope(f"down{r}{p}"):
                         send_down(r, p, pb[r, p] + from_down(r, p))
-                if n >= 3 and ups:
+                if n >= 2 and ups:
                     q, p = ups.pop(0)
                     with scope(f"up{q}{p}"):
                         send_up(q, p, pb[q, p] + from_up(q, p))
@@ -930,18 +935,17 @@
                 dma((2, 2 * T)),
                 dma((2 * T,)),
                 dma((1,)),
-                dma((2, 2 * T, C - 1)),
+                dma((2, T + 1, C - 1)),
                 dma((1,)),
                 dma((1,)),
                 dma((2 * (T - 1), G - 1)),
                 dma((1,)),
                 dma((2 * (T - 1), C - 1)),
                 dma((1,)),
-                dma((T - 2, pieces)),
-                dma((1,)),
-                dma((T - 2, pieces)),
-                dma((1,)),
-                dma((pieces,)),
+                dma((2, pieces)),
+                dma((1,)),
+                dma((2, pieces)),
+                dma((1,)),
                 dma((1,)),
                 dma((pieces, groups - 1)),
                 dma((1,)),

time: 62.1 us -> 61.7 us (level)
  no operation moved by 1% of the time
where the time goes in v6:
time: 61.7 us; the launch traced here: 60.7 us
  Pallas kernels  58.6 us (95%)
  local copies, waits for them, and re-layouts  1.49 us (2%)
  between operations  0.67 us (1%)
    pallas_call x1, Pallas kernels, on_device_fused(): pl.pallas_call(functools.partial(fused_kernel, T, G, C, hp, pieces, group...  58.6 us
    unnamed x3, local copies, waits for them, and re-layouts  1.49 us

profile of v6, /device:TPU:9, one launch (start us, length us, event | category | flops | bytes accessed | tf_op | source)
XLA Modules:
  0.0 60.7 jit_solution(13284286046908656758)
XLA Ops:
  0.7 0.0 copy-start
  0.7 0.6 %copy-done = s32[1,4]{1,0:T(1,128)S(1)} copy-done((s32[1,4]{1,0:T(1,128)S(1)}, s32[1,4]{1,0:T(1,128)}, u32[]{:S(2)}) %copy-start) | copy-done | bytes 40
  1.3 58.6 %shard_map.91 = bf16[256,1280]{1,0:T(8,128)(2,1)S(1)} custom-call(bf16[1,64,3072]{2,1,0:T(8,128)(2,1)} %q_ref.1, bf16[1,64,3072]{2,1,0:T(8,128)(2,1)} %k_ref.1, bf16[1,64,3072]{2,1,0:T(8,128)(2,1)} %v_ref.1, bf16[1,256,1280]{2,1,0:T(8,128)(2,1)} %res_ref.1, bf16[256,1280]{1,0:T(8,128)(2,1)} %fresh_ref.1, bf16[768,1280]{1,0:T(8,128)(2,1)} %w_ref.1, ...), custom_call_target="tpu_custom_call" | custom-call | tf_op jit(solution)/shard_map/pallas_call | solution.py:904
  59.9 0.8 %copy.12 = bf16[1,256,1280]{2,1,0:T(8,128)(2,1)} copy(bf16[1,256,1280]{2,1,0:T(8,128)(2,1)S(1)} %bitcast.1) | data formatting | bytes 1310720
Async XLA Ops:
  0.7 0.7 %copy-start = (s32[1,4]{1,0:T(1,128)S(1)}, s32[1,4]{1,0:T(1,128)}, u32[]{:S(2)}) copy-start(s32[1,4]{1,0:T(1,128)} %mask_ref.1) | copy-start | bytes 52

commit v7 on v6

--- a/solution.py
+++ b/solution.py
@@ -106,7 +106,7 @@
     qb, kv, ab, lb, tb, so, st, mb, fb, gb, wb, w3, twb, rb, pb, down_out, down_in, up_out, up_in,
     load_sem, meta_send, meta_recv, kv_send, q_send, kv_recv, q_recv, pass_send, pass_recv,
     raise_send, ax_send, ax_recv, ac_send, ac_recv, dn_send, dn_recv, up_send, up_recv,
-    w_send, tr_send, tr_recv, near_send, so_send, so_recv, st_send, st_recv,
+    w_send, tr_send, tr_recv, near_send, so_send, so_recv, st_send, st_recv, vh_recv, vp_recv,
 ):
     t = lax.axis_index("tm")
     h = lax.axis_index("head")
@@ -257,6 +257,25 @@
             send_sem=q_send.at[0], recv_sem=q_recv.at[k * T + f], **to(low, h),
         )
 
+    def head_of(j):
+        return slice(j * HD, (j + 1) * HD)
+
+    def value_head(f, j, dx):
+        xx = lax.rem(x + dx, G)
+        column = pl.multiple_of((top * G + xx) * cw + j * HD, HD)
+        return pltpu.make_async_remote_copy(
+            src_ref=v_ref.at[0, :, pl.ds(column, HD)],
+            dst_ref=kv.at[T + f, c, 1, x, :, head_of(j)],
+            send_sem=kv_send.at[0], recv_sem=vh_recv.at[j], **to(low, xx * C + c),
+        )
+
+    def passed_head(i, j, dc):
+        here = kv.at[i, c, 1, :, :, head_of(j)]
+        return pltpu.make_async_remote_copy(
+            src_ref=here, dst_ref=here, send_sem=pass_send.at[0],
+            recv_sem=vp_recv.at[j, dc - 1], **to(t, x * C + lax.rem(c + dc, C)),
+        )
+
     def handed(w):
         return [
             pltpu.make_async_remote_copy(
@@ -283,8 +302,8 @@
     def mine(i, column, size):
         return ab.at[i, c, :, pl.ds(pl.multiple_of(column, HD), size)]
 
-    def across(i, dx):
-        here = mine(i, x * cw, cw)
+    def across(i, dx, j=None):
+        here = mine(i, x * cw, cw) if j is None else mine(i, x * cw + j * HD, HD)
         return pltpu.make_async_remote_copy(
             src_ref=here, dst_ref=here, send_sem=ax_send.at[0], recv_sem=ax_recv.at[i, dx - 1],
             **to(t, lax.rem(x + dx, G) * C + c),
@@ -509,6 +528,36 @@
             for j in range(hp):
                 mix(s, r, j, lb[s, j], tb[s, j])
             share_out(s, r)
+
+        def attend_heads(r):
+            i, n = T + low - 1, T - 1 + r
+
+            def pass_on(j):
+                landed(kv.at[i, c, 1, :, :, head_of(j)], vh_recv.at[j])
+                for dc in range(1, C):
+                    passed_head(i, j, dc).start()
+
+            settle(1, (*range(low - 1), low), (2,))
+            pass_on(0)
+            for j in range(hp):
+                if j + 1 < hp:
+                    pass_on(j + 1)
+                for dc in range(1, C):
+                    landed(
+                        kv.at[i, lax.rem(c + C - dc, C), 1, :, :, head_of(j)],
+                        vp_recv.at[j, dc - 1],
+                    )
+                mix(1, r, j, lb[1, j], tb[1, j])
+                for dx in range(1, G):
+                    across(n, dx, j).start()
+            count["ax"] += G - 1
+            count["passed"] += C - 1
+            if low - 1 < low:
+                raised(i, 2).start()
+                count["raised"] += 1
+            for dc in range(1, C):
+                aside(n, x, dc).start()
+                count["ac"] += 1
 
         def hand_over(s, r):
             i = s * (T - 1) + r
@@ -699,25 +748,27 @@
                     settle(s, range(low + 1), (1,))
                 with scope(f"attend{s}{low - 1}1"):
                     attend_keys(s, low - 1)
-            for s in (0, 1):
-                with scope(f"values{s}"):
-                    take(s, low - 1, (2,))
-                with scope(f"settle{s}2"):
-                    settle(s, range(low + 1), (2,))
-                with scope(f"attend{s}{low - 1}2"):
-                    attend_values(s, low - 1)
+            with scope("values0"):
+                take(0, low - 1, (2,))
+            with scope("settle02"):
+                settle(0, range(low + 1), (2,))
+            with scope("attend02"):
+                attend_values(0, low - 1)
+            with scope("attend12"):
+                attend_heads(low - 1)
             for r in reversed(range(low - 1)):
+                with scope(f"hand0{r + 1}"):
+                    hand_over(0, r + 1)
                 for s in (0, 1):
-                    with scope(f"hand{s}{r + 1}"):
-                        hand_over(s, r + 1)
-                    if s == 1:
-                        for p in range(2):
-                            exchanged(p)
-                        own_parts(r + 1)
                     with scope(f"q{r + 1}{s}"):
                         take_queries(s, r + 1)
                     with scope(f"attend{s}{r}"):
                         attend(s, r)
+                with scope(f"hand1{r + 1}"):
+                    hand_over(1, r + 1)
+                for p in range(2):
+                    exchanged(p)
+                own_parts(r + 1)
             ready = set()
             known = {0, 1} if low > 1 else set()
             swapped = False
@@ -779,7 +830,13 @@
                         count["near"] += 1
             for kind in (1, 2):
                 for w in (low, top):
-                    send((kind,), w)
+                    if kind == 2 and w == top and level == low - 1:
+                        for j in range(hp):
+                            for dx in reversed(range(G)):
+                                value_head(level, j, dx).start()
+                        count["kv"] += G
+                    else:
+                        send((kind,), w)
             for w in (low, top):
                 send((0,), w, (0,))
             for w in range(level + 1, low):
@@ -953,6 +1010,8 @@
                 dma((1,)),
                 dma((1,)),
                 dma((1,)),
+                dma((hp,)),
+                dma((hp, C - 1)),
             ],
             compiler_params=pltpu.CompilerParams(
                 collective_id=0, has_side_effects=True, vmem_limit_bytes=32 * 1024 * 1024

time: 61.7 us -> 61.7 us (level)
  no operation moved by 1% of the time
where the time goes in v7:
time: 61.7 us; the launch traced here: 60.8 us
  Pallas kernels  58.6 us (95%)
  local copies, waits for them, and re-layouts  1.49 us (2%)
  between operations  0.67 us (1%)
    pallas_call x1, Pallas kernels, on_device_fused(): pl.pallas_call(functools.partial(fused_kernel, T, G, C, hp, pieces, group...  58.6 us
    unnamed x3, local copies, waits for them, and re-layouts  1.49 us

profile of v7, /device:TPU:9, one launch (start us, length us, event | category | flops | bytes accessed | tf_op | source)
XLA Modules:
  0.0 60.8 jit_solution(9174005337377667002)
XLA Ops:
  0.7 0.0 copy-start
  0.7 0.6 %copy-done = s32[1,4]{1,0:T(1,128)S(1)} copy-done((s32[1,4]{1,0:T(1,128)S(1)}, s32[1,4]{1,0:T(1,128)}, u32[]{:S(2)}) %copy-start) | copy-done | bytes 40
  1.3 58.6 %shard_map.91 = bf16[256,1280]{1,0:T(8,128)(2,1)S(1)} custom-call(bf16[1,64,3072]{2,1,0:T(8,128)(2,1)} %q_ref.1, bf16[1,64,3072]{2,1,0:T(8,128)(2,1)} %k_ref.1, bf16[1,64,3072]{2,1,0:T(8,128)(2,1)} %v_ref.1, bf16[1,256,1280]{2,1,0:T(8,128)(2,1)} %res_ref.1, bf16[256,1280]{1,0:T(8,128)(2,1)} %fresh_ref.1, bf16[768,1280]{1,0:T(8,128)(2,1)} %w_ref.1, ...), custom_call_target="tpu_custom_call" | custom-call | tf_op jit(solution)/shard_map/pallas_call | solution.py:961
  59.9 0.8 %copy.12 = bf16[1,256,1280]{2,1,0:T(8,128)(2,1)} copy(bf16[1,256,1280]{2,1,0:T(8,128)(2,1)S(1)} %bitcast.1) | data formatting | bytes 1310720
Async XLA Ops:
  0.7 0.7 %copy-start = (s32[1,4]{1,0:T(1,128)S(1)}, s32[1,4]{1,0:T(1,128)}, u32[]{:S(2)}) copy-start(s32[1,4]{1,0:T(1,128)} %mask_ref.1) | copy-start | bytes 52
